TPU v7x, 32 devices: a whole 2x2x4 slice. The times are simulated.
32 devices in a mesh: rep: 4 (over z), shard: 8 (over y, x, core).
Axes of the slice: x: 2, y: 2, z: 4, core: 2. Of those that a mesh axis runs over, the one named last changes fastest.
Arguments:
- tokens: bfloat16 [8192, 2048], P(('rep', 'shard')), may hold values from -6 to 6
- cotangent: bfloat16 [8192, 2048], P(('rep', 'shard')), may hold values from -6 to 6
- placement_order: int32 [4, 8, 2, 128], P('rep', 'shard'), may hold values from 0 to 127, each once within a row
- seq_lengths: int32 [4, 2, 8], P('rep'), may hold values from 0 to 1024, as said below
- ln_gain: bfloat16 [2048], P('shard'), may hold values from 0.25 to 1.75
- ln_bias: bfloat16 [2048], P('shard'), may hold values from -4 to 4
- qkv_weight: bfloat16 [2048, 6144], P('shard'), may hold values from -0.125 to 0.125
- qkv_bias: bfloat16 [6144], P('shard'), may hold values from -6 to 6
- dense_weight: bfloat16 [2048, 2048], P('shard'), may hold values from -2 to 2
- dense_bias: bfloat16 [2048], P('shard'), may hold values from -4 to 4
- fc1_weight: bfloat16 [2048, 8192], P('shard'), may hold values from -0.125 to 0.125
- fc1_bias: bfloat16 [8192], P('shard'), may hold values from -4 to 4
- fc2_weight: bfloat16 [8192, 2048], P('shard'), may hold values from -0.0625 to 0.0625
- fc2_bias: bfloat16 [2048], P('shard'), may hold values from -4 to 4
Outputs:
- mixed: bfloat16 [8192, 2048], P(('rep', 'shard'))
- token_grad: bfloat16 [8192, 2048], P(('rep', 'shard'))
- grad_ln_gain: float32 [2048], P('shard')
- grad_ln_bias: float32 [2048], P('shard')
- grad_qkv_weight: float32 [2048, 6144], P('shard')
- grad_qkv_bias: float32 [6144], P('shard')
- grad_dense_weight: float32 [2048, 2048], P('shard')
- grad_dense_bias: float32 [2048], P('shard')
- grad_fc1_weight: float32 [2048, 8192], P('shard')
- grad_fc1_bias: float32 [8192], P('shard')
- grad_fc2_weight: float32 [8192, 2048], P('shard')
- grad_fc2_bias: float32 [2048], P('shard')
Inputs may be any that keep to these rules, and one draw needn't show every extreme that they name: `seq_lengths`: for replica group r and micro-batch m, entry j is the length of the sequence that starts at block j, or 0 where block j continues the sequence before it. Entry 0 is positive. A sequence that starts at block j runs to the block before the next positive entry (or to the last block), b blocks, and its length is over 128 * (b - 1) and at most 128 * b; b is at most 8; some sequence has 1024 tokens. `placement_order`: each device's row for a micro-batch is a permutation; a value b sends that row to the device of shard index b // 16 of the same replica group.
All inputs are finite; a program needn't handle non-finite values.
Results may differ from a plain program's by a relative error of at most 0.013.
Values may be sent and summed in bfloat16 or wider, within the bound.
A program may use at most 704 MiB of HBM per device.

v0:
```python
import math
import jax
import jax.numpy as jnp
from jax import lax
from jax.sharding import PartitionSpec as P

HEADS = 32
HDIM = 64
ROT = 32
BLOCK = 128
MICRO = 2
MAXBLK = 8


def shifted(block, axis, distance):
    devices = range(lax.axis_size(axis))
    route = [(i - distance, i) for i in devices if i - distance in devices]
    return lax.ppermute(block, axis, route)


def contract_last(left, right):
    return lax.dot_general(
        left, right, (((1,), (1,)), ((), ())), preferred_element_type=jnp.float32
    )


def contract_first(left, right):
    return lax.dot_general(
        left, right, (((0,), (0,)), ((), ())), preferred_element_type=jnp.float32
    )


def normalize(inputs, gain_vec, bias_vec):
    average = jnp.mean(inputs, axis=-1, keepdims=True)
    centered = inputs - average
    variance = jnp.mean(centered * centered, axis=-1, keepdims=True)
    return centered * lax.rsqrt(variance + 1e-05) * gain_vec + bias_vec


def rotary_tables(position):
    half_dim = ROT // 2
    freqs = jnp.exp(-math.log(10000.0) * jnp.arange(half_dim, dtype=jnp.float32) * 2.0 / ROT)
    angles = position.astype(jnp.float32)[:, None] * freqs[None, :]
    angles = jnp.concatenate([angles, angles], axis=1)
    return (jnp.cos(angles)[:, None, :], jnp.sin(angles)[:, None, :])


def rotate(heads, cosine_table, sine_table):
    half_dim = ROT // 2
    turned_part = heads[..., :ROT]
    swapped = jnp.concatenate([-turned_part[..., half_dim:], turned_part[..., :half_dim]], axis=-1)
    return jnp.concatenate(
        [turned_part * cosine_table + swapped * sine_table, heads[..., ROT:]], axis=-1
    )


def gelu_tanh(values):
    return jax.nn.gelu(values, approximate=True)


def block_meta(lengths_row, first_row, span_rows):
    block_count = lengths_row.shape[0]
    blocks = jnp.arange(block_count, dtype=jnp.int32)
    begins = jnp.max(
        jnp.where(
            (lengths_row[None, :] > 0) & (blocks[None, :] <= blocks[:, None]), blocks[None, :], 0
        ),
        axis=1,
    )
    begin_length = jnp.sum(
        jnp.where(begins[:, None] == blocks[None, :], lengths_row[None, :], 0), axis=1
    )
    global_rows = first_row + jnp.arange(span_rows, dtype=jnp.int32)
    picks = (global_rows // BLOCK)[:, None] == blocks[None, :]
    segment = jnp.sum(jnp.where(picks, begins[None, :], 0), axis=1)
    limit = jnp.sum(jnp.where(picks, begin_length[None, :], 0), axis=1)
    position = global_rows - segment * BLOCK
    usable = (global_rows >= 0) & (position < limit)
    return (segment, position, usable)


def reduce_grads(hn_rows, dqkv_rows, dup_rows, ob_rows, gact_rows, gy_rows, vectors):
    wide = lax.psum_scatter(
        jnp.concatenate(
            [
                contract_first(hn_rows, dqkv_rows),
                contract_first(hn_rows, dup_rows),
                contract_first(ob_rows, gy_rows),
            ],
            axis=1,
        ).astype(jnp.bfloat16),
        "shard",
        scatter_dimension=0,
        tiled=True,
    ).astype(jnp.float32)
    deep = lax.psum_scatter(
        contract_first(gact_rows, gy_rows).astype(jnp.bfloat16),
        "shard",
        scatter_dimension=0,
        tiled=True,
    ).astype(jnp.float32)
    scattered = (
        lax.psum_scatter(
            vectors[0].astype(jnp.bfloat16), "shard", scatter_dimension=0, tiled=True
        ).astype(jnp.float32),
        lax.psum_scatter(
            vectors[1].astype(jnp.bfloat16), "shard", scatter_dimension=0, tiled=True
        ).astype(jnp.float32),
        lax.psum_scatter(
            vectors[2].astype(jnp.bfloat16), "shard", scatter_dimension=0, tiled=True
        ).astype(jnp.float32),
        lax.psum_scatter(
            vectors[3].astype(jnp.bfloat16), "shard", scatter_dimension=0, tiled=True
        ).astype(jnp.float32),
        lax.psum_scatter(
            vectors[4].astype(jnp.bfloat16), "shard", scatter_dimension=0, tiled=True
        ).astype(jnp.float32),
    )
    return lax.psum(
        (wide, deep, scattered[0], scattered[1], scattered[2], scattered[3], scattered[4]), "rep"
    )


def body(
    tokens,
    cotangent,
    placement_order,
    seq_lengths,
    ln_gain,
    ln_bias,
    qkv_weight,
    qkv_bias,
    dense_weight,
    dense_bias,
    fc1_weight,
    fc1_bias,
    fc2_weight,
    fc2_bias,
):
    group_size = lax.axis_size("shard")
    shard_pos = lax.axis_index("shard")
    model_width = tokens.shape[1]
    ff_width = fc1_weight.shape[1]
    row_count = tokens.shape[0] // MICRO
    cap_rows = row_count // group_size
    blk_dev = row_count // BLOCK
    reach = (MAXBLK - 1 + blk_dev - 1) // blk_dev
    span_rows = (reach + 1) * row_count
    scale = 1.0 / math.sqrt(HDIM)
    orders = placement_order[0, 0]
    micro_ids = jnp.arange(MICRO, dtype=jnp.int32)[:, None]
    spots = jnp.broadcast_to(jnp.arange(row_count, dtype=jnp.int32)[None, :], orders.shape)
    inverse = jnp.zeros_like(orders).at[micro_ids, orders].set(spots)

    def to_buffer(array):
        return jnp.take_along_axis(
            array.reshape(MICRO, row_count, model_width), inverse[:, :, None], axis=1
        ).reshape(MICRO, group_size, cap_rows, model_width)

    arrived = (
        lax.all_to_all(to_buffer(tokens), "shard", split_axis=1, concat_axis=1, tiled=True),
        lax.all_to_all(to_buffer(cotangent), "shard", split_axis=1, concat_axis=1, tiled=True),
    )
    att_x = arrived[0].reshape(MICRO, row_count, model_width)
    att_g = arrived[1].reshape(MICRO, row_count, model_width)
    shards = (
        ln_gain,
        ln_bias,
        qkv_weight,
        qkv_bias,
        dense_weight,
        dense_bias,
        fc1_weight,
        fc1_bias,
        fc2_weight,
        fc2_bias,
    )
    gathered_once = (
        lax.all_gather(shards[0], "shard", axis=0, tiled=True),
        lax.all_gather(shards[1], "shard", axis=0, tiled=True),
        lax.all_gather(shards[2], "shard", axis=0, tiled=True),
        lax.all_gather(shards[3], "shard", axis=0, tiled=True),
        lax.all_gather(shards[4], "shard", axis=0, tiled=True),
        lax.all_gather(shards[5], "shard", axis=0, tiled=True),
        lax.all_gather(shards[6], "shard", axis=0, tiled=True),
        lax.all_gather(shards[7], "shard", axis=0, tiled=True),
        lax.all_gather(shards[8], "shard", axis=0, tiled=True),
        lax.all_gather(shards[9], "shard", axis=0, tiled=True),
    )
    mixed_list = []
    grad_list = []
    stored = []
    totals = None
    for micro_idx in range(MICRO):
        gain_full, lnb_full, w_qkv, b_qkv, w_dense, b_dense, w_fc1, b_fc1, w_fc2, b_fc2 = (
            gathered_once
        )
        segment, position, usable = block_meta(
            seq_lengths[0, micro_idx], (shard_pos - reach) * row_count, span_rows
        )
        seg_query = segment[reach * row_count :]
        pos_query = position[reach * row_count :]
        valid_query = usable[reach * row_count :]
        inputs = att_x[micro_idx].astype(jnp.float32)
        normed, norm_pull = jax.vjp(
            normalize, inputs, gain_full.astype(jnp.float32), lnb_full.astype(jnp.float32)
        )
        hn_rows = normed.astype(jnp.bfloat16)
        qkv = jnp.dot(hn_rows, w_qkv, preferred_element_type=jnp.float32) + b_qkv.astype(
            jnp.float32
        )
        queries = qkv[:, :model_width].reshape(row_count, HEADS, HDIM)
        keys_raw = qkv[:, model_width : 2 * model_width].reshape(row_count, HEADS, HDIM)
        value_rows = qkv[:, 2 * model_width :].astype(jnp.bfloat16)
        cosine_table, sine_table = rotary_tables(pos_query)
        turned, turn_pull = jax.vjp(
            lambda first, second: (
                rotate(first, cosine_table, sine_table),
                rotate(second, cosine_table, sine_table),
            ),
            queries,
            keys_raw,
        )
        q_low = turned[0].astype(jnp.bfloat16)
        key_rows = turned[1].astype(jnp.bfloat16).reshape(row_count, model_width)
        older = []
        for shift_by in range(1, reach + 1):
            older.append(shifted((key_rows, value_rows), "shard", shift_by))
        key_win = jnp.concatenate(
            [received[0] for received in reversed(older)] + [key_rows], axis=0
        ).reshape(span_rows, HEADS, HDIM)
        val_win = jnp.concatenate(
            [received[1] for received in reversed(older)] + [value_rows], axis=0
        ).reshape(span_rows, HEADS, HDIM)
        allowed = (
            (seg_query[:, None] == segment[None, :])
            & (position[None, :] <= pos_query[:, None])
            & usable[None, :]
        )
        scores = (
            jnp.einsum("qhd,khd->hqk", q_low, key_win, preferred_element_type=jnp.float32) * scale
        )
        masked = jnp.where(allowed[None], scores, -1e30)
        top_score = jnp.max(masked, axis=-1, keepdims=True)
        expo = jnp.exp(masked - top_score)
        denom = jnp.sum(expo, axis=-1, keepdims=True)
        log_total = top_score + jnp.log(denom)
        probs = expo / denom
        attn_rows = jnp.einsum(
            "hqk,khd->qhd", probs.astype(jnp.bfloat16), val_win, preferred_element_type=jnp.float32
        )
        ob_rows = attn_rows.reshape(row_count, model_width).astype(jnp.bfloat16)
        attn_proj = jnp.dot(ob_rows, w_dense, preferred_element_type=jnp.float32) + b_dense.astype(
            jnp.float32
        )
        upper = jnp.dot(hn_rows, w_fc1, preferred_element_type=jnp.float32) + b_fc1.astype(
            jnp.float32
        )
        activated, gelu_pull = jax.vjp(gelu_tanh, upper)
        gact_rows = activated.astype(jnp.bfloat16)
        mlp_out = jnp.dot(gact_rows, w_fc2, preferred_element_type=jnp.float32) + b_fc2.astype(
            jnp.float32
        )
        mixed_rows = inputs + jnp.where(valid_query[:, None], attn_proj + mlp_out, 0.0)
        mixed_list.append(mixed_rows.astype(jnp.bfloat16))
        gy_rows = jnp.where(valid_query[:, None], att_g[micro_idx], jnp.zeros((), jnp.bfloat16))
        d_act = contract_last(gy_rows, w_fc2)
        dup_rows = gelu_pull(d_act)[0].astype(jnp.bfloat16)
        d_out = contract_last(gy_rows, w_dense).astype(jnp.bfloat16).reshape(row_count, HEADS, HDIM)
        again = (
            jnp.einsum("qhd,khd->hqk", q_low, key_win, preferred_element_type=jnp.float32) * scale
        )
        probs_again = jnp.where(allowed[None], jnp.exp(again - log_total), 0.0)
        d_probs = jnp.einsum("qhd,khd->hqk", d_out, val_win, preferred_element_type=jnp.float32)
        row_delta = jnp.sum(probs_again * d_probs, axis=-1, keepdims=True)
        d_scores = (probs_again * (d_probs - row_delta)).astype(jnp.bfloat16)
        d_query = (
            jnp.einsum("hqk,khd->qhd", d_scores, key_win, preferred_element_type=jnp.float32)
            * scale
        )
        d_keywin = (
            jnp.einsum("hqk,qhd->khd", d_scores, q_low, preferred_element_type=jnp.float32) * scale
        ).reshape(span_rows, model_width)
        d_valwin = jnp.einsum(
            "hqk,qhd->khd",
            probs_again.astype(jnp.bfloat16),
            d_out,
            preferred_element_type=jnp.float32,
        ).reshape(span_rows, model_width)
        key_total = d_keywin[reach * row_count :]
        value_total = d_valwin[reach * row_count :]
        for shift_by in range(1, reach + 1):
            lower_row = (reach - shift_by) * row_count
            returned = (
                shifted(
                    d_keywin[lower_row : lower_row + row_count].astype(jnp.bfloat16),
                    "shard",
                    -shift_by,
                ).astype(jnp.float32),
                shifted(
                    d_valwin[lower_row : lower_row + row_count].astype(jnp.bfloat16),
                    "shard",
                    -shift_by,
                ).astype(jnp.float32),
            )
            key_total = key_total + returned[0]
            value_total = value_total + returned[1]
        unturned = turn_pull((d_query, key_total.reshape(row_count, HEADS, HDIM)))
        dqkv_rows = jnp.concatenate(
            [
                unturned[0].reshape(row_count, model_width),
                unturned[1].reshape(row_count, model_width),
                value_total,
            ],
            axis=1,
        ).astype(jnp.bfloat16)
        d_normed = contract_last(dqkv_rows, w_qkv) + contract_last(dup_rows, w_fc1)
        d_inputs, d_gain, d_lnbias = norm_pull(d_normed)
        grad_list.append((att_g[micro_idx].astype(jnp.float32) + d_inputs).astype(jnp.bfloat16))
        vectors = (
            jnp.sum(dqkv_rows.astype(jnp.float32), axis=0),
            jnp.sum(dup_rows.astype(jnp.float32), axis=0),
            jnp.sum(gy_rows.astype(jnp.float32), axis=0),
            d_gain,
            d_lnbias,
        )
        stored.append((hn_rows, dqkv_rows, dup_rows, ob_rows, gact_rows, gy_rows, vectors))
    joined = [jnp.concatenate([entry[slot] for entry in stored], axis=0) for slot in range(6)]
    vector_sums = tuple(
        (jnp.sum(jnp.stack([entry[6][slot] for entry in stored]), axis=0) for slot in range(5))
    )
    totals = reduce_grads(
        joined[0], joined[1], joined[2], joined[3], joined[4], joined[5], vector_sums
    )
    mixed_back = jnp.stack(mixed_list).reshape(MICRO, group_size, cap_rows, model_width)
    grads_back = jnp.stack(grad_list).reshape(MICRO, group_size, cap_rows, model_width)
    homeward = (
        lax.all_to_all(mixed_back, "shard", split_axis=1, concat_axis=1, tiled=True),
        lax.all_to_all(grads_back, "shard", split_axis=1, concat_axis=1, tiled=True),
    )

    def from_buffer(array):
        return jnp.take_along_axis(
            array.reshape(MICRO, row_count, model_width), orders[:, :, None], axis=1
        ).reshape(MICRO * row_count, model_width)

    wide, deep, bias_qkv, bias_fc1, bias_out, gain_grad, lnbias_grad = totals
    qkv_cols = 3 * model_width
    return (
        from_buffer(homeward[0]),
        from_buffer(homeward[1]),
        gain_grad,
        lnbias_grad,
        wide[:, :qkv_cols],
        bias_qkv,
        wide[:, qkv_cols + ff_width :],
        bias_out,
        wide[:, qkv_cols : qkv_cols + ff_width],
        bias_fc1,
        deep,
        bias_out,
    )


def solution(mesh):
    placed = (
        P(("rep", "shard"), None),
        P(("rep", "shard"), None),
        P("rep", "shard", None, None),
        P("rep", None, None),
        P("shard"),
        P("shard"),
        P("shard", None),
        P("shard"),
        P("shard", None),
        P("shard"),
        P("shard", None),
        P("shard"),
        P("shard", None),
        P("shard"),
    )
    return jax.shard_map(
        body,
        mesh=mesh,
        in_specs=placed,
        out_specs=(
            P(("rep", "shard"), None),
            P(("rep", "shard"), None),
            P("shard"),
            P("shard"),
            P("shard", None),
            P("shard"),
            P("shard", None),
            P("shard"),
            P("shard", None),
            P("shard"),
            P("shard", None),
            P("shard"),
        ),
        check_vma=False,
    )
```

profile of v0, /device:TPU:0, one launch (start us, length us, event | category | flops | bytes accessed | tf_op | source)
XLA Modules:
  0.0 2567.9 jit_solution(3848046647579262749)
XLA Ops:
  10.6 11.4 scatter_fusion
  32.2 5.2 all-to-all-start
  39.3 24.7 all-gather.1
  64.0 9.3 all-gather
  73.4 7.7 all_gather.37
  81.1 9.2 all-gather.2
  96.2 10.5 reduce-scatter.5.cloned.1.call-start
  108.4 14.7 all-to-all-done.2
  125.6 6.6 convolution_convert_fusion.5
  133.3 6.3 convolution_convert_fusion.4
  140.6 74.5 %all-gather.10.cloned.1.call-done = bf16[2048,6144]{1,0:T(8,128)(2,1)} async-done(((bf16[256,6144]{1,0:T(8,128)(2,1)}), bf16[2048,6144]{1,0:T(8,128)(2,1)}) %all-gather.10.cloned.1.call-update) | async-done | bytes 25165840 | tf_op jit(solution)/shard_map/all_gather | solution.py:181
  215.1 10.0 convolution_add_fusion.3
  230.2 147.6 %all-gather.16.cloned.1.call-done = bf16[8192,2048]{1,0:T(8,128)(2,1)} async-done(((bf16[1024,2048]{1,0:T(8,128)(2,1)}), bf16[8192,2048]{1,0:T(8,128)(2,1)}) %all-gather.16.cloned.1.call-update) | async-done | bytes 33554448 | tf_op jit(solution)/shard_map/all_gather | solution.py:187
  377.8 19.8 fusion.171
  397.6 17.4 fusion.172
  415.0 125.3 %all-gather.14.cloned.1.call-done = bf16[2048,8192]{1,0:T(8,128)(2,1)} async-done(((bf16[256,8192]{1,0:T(8,128)(2,1)}), bf16[2048,8192]{1,0:T(8,128)(2,1)}) %all-gather.14.cloned.1.call-update) | async-done | bytes 33554448 | tf_op jit(solution)/shard_map/all_gather | solution.py:185
  540.4 18.5 convert_reduce_fusion.1
  558.9 18.6 convert_reduce_fusion
  577.5 16.2 convolution_convert_fusion
  609.5 14.5 convolution_add_fusion.2
  639.4 7.1 collective-permute-start.5
  668.0 65.2 %collective-permute-done = bf16[128,2048]{1,0:T(8,128)(2,1)S(1)} collective-permute-done((bf16[128,2048]{1,0:T(8,128)(2,1)S(1)}, bf16[128,2048]{1,0:T(8,128)(2,1)S(1)}, u32[]{:S(2)}, u32[]{:S(2)}) %collective-permute-start) | collective-permute-done | bytes 524320 | tf_op jit(solution)/shard_map/ppermute | solution.py:18
  737.5 7.5 collective-permute-start.19
  745.8 17.1 collective-permute-done.3
  774.4 54.3 %collective-permute-done.14 = bf16[128,2048]{1,0:T(8,128)(2,1)S(1)} collective-permute-done((bf16[128,2048]{1,0:T(8,128)(2,1)S(1)}, bf16[128,2048]{1,0:T(8,128)(2,1)S(1)}, u32[]{:S(2)}, u32[]{:S(2)}) %collective-permute-start.14) | collective-permute-done | bytes 524320 | tf_op jit(solution)/shard_map/ppermute | solution.py:18
  833.8 5.5 collective-permute-start.25
  840.2 16.6 collective-permute-done.17
  856.8 5.3 collective-permute-start.24
  862.9 6.6 copy.93
  880.1 13.6 multiply_reduce_fusion.1
  893.7 13.5 multiply_convert_fusion.1
  915.4 10.4 fusion.167
  935.2 6.4 copy.96
  970.8 9.1 fusion.169
  981.0 13.7 multiply_reduce_fusion
  994.7 13.9 multiply_convert_fusion
  1014.4 5.3 fusion.64
  1020.8 7.8 fusion.63
  1028.8 6.7 fusion.66
  1035.5 9.8 fusion.65
  1045.3 5.8 convolution_convert_fusion.3
  1062.2 6.0 collective-permute-done.30
  1077.1 20.7 collective-permute-done.48
  1104.7 16.7 collective-permute-done.44
  1124.8 23.6 collective-permute-done.41
  1167.7 25.6 collective-permute-done.55
  1197.2 13.6 collective-permute-done.52
  1212.2 15.1 convolution_convert_fusion.2
  1227.4 15.5 convolution_convert_fusion.1
  1242.9 44.7 %pad_maximum_fusion = bf16[2048,16384]{1,0:T(8,128)(2,1)} fusion(bf16[2048,2048]{1,0:T(8,128)(2,1)} %convolution_convert_fusion.3, bf16[2048,8192]{1,0:T(8,128)(2,1)} %convolution_convert_fusion.1, bf16[2048,6144]{1,0:T(8,128)(2,1)} %convolution_convert_fusion.2), kind=kLoop, calls=%fused_computation.5 | loop fusion | flops 201326592 | bytes 134217728 | tf_op jit(solution)/shard_map/concatenate | solution.py:84
  1291.0 17.5 all-gather.4
  1308.5 9.6 all-gather.3
  1320.2 7.2 convolution_add_fusion.9
  1327.4 7.3 convolution_add_fusion.8
  1335.8 22.8 fusion.97
  1358.6 18.7 fusion.96
  1377.3 19.1 fusion.61
  1396.4 15.1 fusion.62
  1418.2 17.5 convolution_add_fusion.4
  1435.8 19.7 multiply_reduce_fusion.3
  1462.0 45.2 %all-reduce.22 = (bf16[2048]{0:T(1024)(128)(2,1)S(1)}, bf16[2048]{0:T(1024)(128)(2,1)S(1)}, bf16[6144]{0:T(1024)(128)(2,1)S(1)}, bf16[2048]{0:T(1024)(128)(2,1)S(1)}, bf16[8192]{0:T(1024)(128)(2,1)S(1)}) all-reduce(bf16[2048]{0:T(1024)(128)(2,1)S(1)} %add_convert_fusion.12, ...), channel_id=2, replica_groups=mesh['rep'=4,'shard'=8] {'shard'}, use_global_device_ids=true, to_apply=%region_25.27.clone | all-reduce | flops 20480 | bytes 81920
  1519.2 186.8 %reduce-scatter.3.cloned.1.call-done = bf16[256,16384]{1,0:T(8,128)(2,1)} async-done(((bf16[2048,16384]{1,0:T(8,128)(2,1)}), bf16[256,16384]{1,0:T(8,128)(2,1)}) %reduce-scatter.3.cloned.1.call-update) | async-done | bytes 8388624 | tf_op jit(solution)/shard_map/reduce_scatter | solution.py:83
  1706.0 840.0 %all-reduce.24 = (f32[256]{0:T(256)}, f32[256]{0:T(256)}, f32[256,16384]{1,0:T(8,128)}, f32[768]{0:T(1024)}, f32[256]{0:T(256)S(1)}, /*index=5*/f32[1024]{0:T(1024)}, f32[1024,2048]{1,0:T(8,128)}) all-reduce(f32[256]{0:T(256)S(1)} %dynamic-slice_convert_fusion.4, ...), channel_id=1, replica_groups=mesh['rep'=4,'shard'=8] {'rep'}, use_global_device_ids=true, to_apply=%region_26.28 | all-reduce | flops 6294016 | bytes 37769216 | tf_op jit(solution)/shard_map/psum | solution.py:119
  2549.3 6.9 slice.442
  (570 shorter events, 264.7 us)
Async XLA Ops:
  7.2 118.4 %all-gather.12.cloned.1.call-start = ((), (), s32[]{:S(2)}) async-start(), calls=%async_computation.7 | async-start | bytes 9437184 | tf_op jit(solution)/shard_map/all_gather | solution.py:183
  7.9 207.1 %all-gather.10.cloned.1.call-start = ((), (), s32[]{:S(2)}) async-start(), calls=%async_computation.6 | async-start | bytes 28311552 | tf_op jit(solution)/shard_map/all_gather | solution.py:181
  8.7 369.1 %all-gather.16.cloned.1.call-start = ((), (), s32[]{:S(2)}) async-start(), calls=%async_computation.9 | async-start | bytes 37748736 | tf_op jit(solution)/shard_map/all_gather | solution.py:187
  9.4 530.9 %all-gather.14.cloned.1.call-start = ((), (), s32[]{:S(2)}) async-start(), calls=%async_computation.8 | async-start | bytes 37748736 | tf_op jit(solution)/shard_map/all_gather | solution.py:185
  32.2 60.5 %all-to-all-start = ((bf16[2,8,16,2048]{3,2,0,1:T(8,128)(2,1)}), bf16[2,8,16,2048]{3,2,0,1:T(8,128)(2,1)S(1)}, u32[]{:S(2)}, u32[]{:S(2)}) async-start(bf16[2,8,16,2048]{3,2,0,1:T(8,128)(2,1)} %copy.92), calls=%async_computation | async-start | bytes 2097152 | tf_op jit(solution)/shard_map/all_to_all | solution.py:161
  92.6 30.4 %all-to-all-start.2 = ((bf16[2,8,16,2048]{3,2,0,1:T(8,128)(2,1)}), bf16[2,8,16,2048]{3,2,0,1:T(8,128)(2,1)S(1)}, u32[]{:S(2)}, u32[]{:S(2)}) async-start(bf16[2,8,16,2048]{3,2,0,1:T(8,128)(2,1)} %copy.102), calls=%async_computation.2 | async-start | bytes 2097152 | tf_op jit(solution)/shard_map/all_to_all | solution.py:162
  96.2 1423.0 %reduce-scatter.5.cloned.1.call-start = ((), (), s32[]{:S(2)}) async-start(), calls=%async_computation.11 | async-start | bytes 37748736 | tf_op jit(solution)/shard_map/reduce_scatter | solution.py:96
  593.8 1112.2 %reduce-scatter.3.cloned.1.call-start = ((), (), s32[]{:S(2)}) async-start(), calls=%async_computation.10 | async-start | bytes 75497472 | tf_op jit(solution)/shard_map/reduce_scatter | solution.py:83
  595.0 55.4 %collective-permute-start.11 = (bf16[128,2048]{0,1:T(8,128)(2,1)}, bf16[128,2048]{0,1:T(8,128)(2,1)}, u32[]{:S(2)}, u32[]{:S(2)}) collective-permute-start(bf16[128,2048]{0,1:T(8,128)(2,1)} %bitcast.18), channel_id=1, source_target_pairs={{0,3},{1,4},{2,5},{3,6},{4,7},{8,11},{9,12},{10,13},{11,14},{12,15... | collective-permute-start | bytes 1572872 | tf_op jit(solution)/shard_map/ppermute | solution.py:18
  599.0 48.8 %collective-permute-start.10 = (bf16[128,2048]{0,1:T(8,128)(2,1)}, bf16[128,2048]{0,1:T(8,128)(2,1)}, u32[]{:S(2)}, u32[]{:S(2)}) collective-permute-start(bf16[128,2048]{0,1:T(8,128)(2,1)} %bitcast.18), channel_id=1, source_target_pairs={{0,4},{1,5},{2,6},{3,7},{8,12},{9,13},{10,14},{11,15},{16,20},{17,... | collective-permute-start | bytes 1572872 | tf_op jit(solution)/shard_map/ppermute | solution.py:18
  601.5 38.0 %collective-permute-start.9 = (bf16[128,2048]{0,1:T(8,128)(2,1)}, bf16[128,2048]{0,1:T(8,128)(2,1)}, u32[]{:S(2)}, u32[]{:S(2)}) collective-permute-start(bf16[128,2048]{0,1:T(8,128)(2,1)} %bitcast.18), channel_id=1, source_target_pairs={{0,5},{1,6},{2,7},{8,13},{9,14},{10,15},{16,21},{17,22},{18,23},{2... | collective-permute-start | bytes 1572872 | tf_op jit(solution)/shard_map/ppermute | solution.py:18
  603.6 33.2 %collective-permute-start.8 = (bf16[128,2048]{0,1:T(8,128)(2,1)}, bf16[128,2048]{0,1:T(8,128)(2,1)}, u32[]{:S(2)}, u32[]{:S(2)}) collective-permute-start(bf16[128,2048]{0,1:T(8,128)(2,1)} %bitcast.18), channel_id=1, source_target_pairs={{0,6},{1,7},{8,14},{9,15},{16,22},{17,23},{24,30},{25,31}} | collective-permute-start | bytes 1572872 | tf_op jit(solution)/shard_map/ppermute | solution.py:18
  605.7 28.4 %collective-permute-start.7 = (bf16[128,2048]{0,1:T(8,128)(2,1)}, bf16[128,2048]{0,1:T(8,128)(2,1)}, u32[]{:S(2)}, u32[]{:S(2)}) collective-permute-start(bf16[128,2048]{0,1:T(8,128)(2,1)} %bitcast.18), channel_id=1, source_target_pairs={{0,7},{8,15},{16,23},{24,31}} | collective-permute-start | bytes 1572872 | tf_op jit(solution)/shard_map/ppermute | solution.py:18
  634.1 21.2 collective-permute-start.12
  636.8 20.0 collective-permute-start.13
  639.4 128.6 %collective-permute-start.5 = (bf16[128,2048]{1,0:T(8,128)(2,1)S(1)}, bf16[128,2048]{1,0:T(8,128)(2,1)S(1)}, u32[]{:S(2)}, u32[]{:S(2)}) collective-permute-start(bf16[128,2048]{1,0:T(8,128)(2,1)S(1)} %slice.522), channel_id=1, source_target_pairs={{0,2},{1,3},{2,4},{3,5},{4,6},{5,7},{8,10},{9,11},{10,12},{11,13},... | collective-permute-start | bytes 1572872 | tf_op jit(solution)/shard_map/ppermute | solution.py:18
  647.8 118.1 %collective-permute-start.4 = (bf16[128,2048]{1,0:T(8,128)(2,1)S(1)}, bf16[128,2048]{1,0:T(8,128)(2,1)S(1)}, u32[]{:S(2)}, u32[]{:S(2)}) collective-permute-start(bf16[128,2048]{1,0:T(8,128)(2,1)S(1)} %slice.522), channel_id=1, source_target_pairs={{0,3},{1,4},{2,5},{3,6},{4,7},{8,11},{9,12},{10,13},{11,14},{12,15... | collective-permute-start | bytes 1572872 | tf_op jit(solution)/shard_map/ppermute | solution.py:18
  650.4 87.1 %collective-permute-start.2 = (bf16[128,2048]{1,0:T(8,128)(2,1)S(1)}, bf16[128,2048]{1,0:T(8,128)(2,1)S(1)}, u32[]{:S(2)}, u32[]{:S(2)}) collective-permute-start(bf16[128,2048]{1,0:T(8,128)(2,1)S(1)} %slice.522), channel_id=1, source_target_pairs={{0,5},{1,6},{2,7},{8,13},{9,14},{10,15},{16,21},{17,22},{18,23},{2... | collective-permute-start | bytes 1572872 | tf_op jit(solution)/shard_map/ppermute | solution.py:18
  655.3 80.0 %collective-permute-start.1 = (bf16[128,2048]{1,0:T(8,128)(2,1)S(1)}, bf16[128,2048]{1,0:T(8,128)(2,1)S(1)}, u32[]{:S(2)}, u32[]{:S(2)}) collective-permute-start(bf16[128,2048]{1,0:T(8,128)(2,1)S(1)} %slice.522), channel_id=1, source_target_pairs={{0,6},{1,7},{8,14},{9,15},{16,22},{17,23},{24,30},{25,31}} | collective-permute-start | bytes 1572872 | tf_op jit(solution)/shard_map/ppermute | solution.py:18
  656.9 76.3 %collective-permute-start = (bf16[128,2048]{1,0:T(8,128)(2,1)S(1)}, bf16[128,2048]{1,0:T(8,128)(2,1)S(1)}, u32[]{:S(2)}, u32[]{:S(2)}) collective-permute-start(bf16[128,2048]{1,0:T(8,128)(2,1)S(1)} %slice.522), channel_id=1, source_target_pairs={{0,7},{8,15},{16,23},{24,31}} | collective-permute-start | bytes 1572872 | tf_op jit(solution)/shard_map/ppermute | solution.py:18
  733.2 29.7 %collective-permute-start.3 = (bf16[128,2048]{1,0:T(8,128)(2,1)S(1)}, bf16[128,2048]{1,0:T(8,128)(2,1)S(1)}, u32[]{:S(2)}, u32[]{:S(2)}) collective-permute-start(bf16[128,2048]{1,0:T(8,128)(2,1)S(1)} %slice.522), channel_id=1, source_target_pairs={{0,4},{1,5},{2,6},{3,7},{8,12},{9,13},{10,14},{11,15},{16,20},{17,... | collective-permute-start | bytes 1572872 | tf_op jit(solution)/shard_map/ppermute | solution.py:18
  735.3 34.8 %collective-permute-start.6 = (bf16[128,2048]{1,0:T(8,128)(2,1)S(1)}, bf16[128,2048]{1,0:T(8,128)(2,1)S(1)}, u32[]{:S(2)}, u32[]{:S(2)}) collective-permute-start(bf16[128,2048]{1,0:T(8,128)(2,1)S(1)} %slice.522), channel_id=1, source_target_pairs={{0,1},{1,2},{2,3},{3,4},{4,5},{5,6},{6,7},{8,9},{9,10},{10,11},{11... | collective-permute-start | bytes 1572872 | tf_op jit(solution)/shard_map/ppermute | solution.py:18
  737.5 135.9 %collective-permute-start.19 = (bf16[128,2048]{1,0:T(8,128)(2,1)S(1)}, bf16[128,2048]{1,0:T(8,128)(2,1)}, u32[]{:S(2)}, u32[]{:S(2)}) collective-permute-start(bf16[128,2048]{1,0:T(8,128)(2,1)S(1)} %slice.521), channel_id=1, source_target_pairs={{0,2},{1,3},{2,4},{3,5},{4,6},{5,7},{8,10},{9,11},{10,12},{11,13},... | collective-permute-start | bytes 1572872 | tf_op jit(solution)/shard_map/ppermute | solution.py:18
  762.9 106.5 %collective-permute-start.18 = (bf16[128,2048]{1,0:T(8,128)(2,1)S(1)}, bf16[128,2048]{1,0:T(8,128)(2,1)}, u32[]{:S(2)}, u32[]{:S(2)}) collective-permute-start(bf16[128,2048]{1,0:T(8,128)(2,1)S(1)} %slice.521), channel_id=1, source_target_pairs={{0,3},{1,4},{2,5},{3,6},{4,7},{8,11},{9,12},{10,13},{11,14},{12,15... | collective-permute-start | bytes 1572872 | tf_op jit(solution)/shard_map/ppermute | solution.py:18
  765.9 68.0 %collective-permute-start.16 = (bf16[128,2048]{1,0:T(8,128)(2,1)S(1)}, bf16[128,2048]{1,0:T(8,128)(2,1)S(1)}, u32[]{:S(2)}, u32[]{:S(2)}) collective-permute-start(bf16[128,2048]{1,0:T(8,128)(2,1)S(1)} %slice.521), channel_id=1, source_target_pairs={{0,5},{1,6},{2,7},{8,13},{9,14},{10,15},{16,21},{17,22},{18,23},{2... | collective-permute-start | bytes 1572872 | tf_op jit(solution)/shard_map/ppermute | solution.py:18
  768.0 62.9 %collective-permute-start.15 = (bf16[128,2048]{1,0:T(8,128)(2,1)S(1)}, bf16[128,2048]{1,0:T(8,128)(2,1)S(1)}, u32[]{:S(2)}, u32[]{:S(2)}) collective-permute-start(bf16[128,2048]{1,0:T(8,128)(2,1)S(1)} %slice.521), channel_id=1, source_target_pairs={{0,6},{1,7},{8,14},{9,15},{16,22},{17,23},{24,30},{25,31}} | collective-permute-start | bytes 1572872 | tf_op jit(solution)/shard_map/ppermute | solution.py:18
  770.2 58.6 %collective-permute-start.14 = (bf16[128,2048]{1,0:T(8,128)(2,1)S(1)}, bf16[128,2048]{1,0:T(8,128)(2,1)S(1)}, u32[]{:S(2)}, u32[]{:S(2)}) collective-permute-start(bf16[128,2048]{1,0:T(8,128)(2,1)S(1)} %slice.521), channel_id=1, source_target_pairs={{0,7},{8,15},{16,23},{24,31}} | collective-permute-start | bytes 1572872 | tf_op jit(solution)/shard_map/ppermute | solution.py:18
  828.7 28.0 %collective-permute-start.17 = (bf16[128,2048]{1,0:T(8,128)(2,1)S(1)}, bf16[128,2048]{1,0:T(8,128)(2,1)S(1)}, u32[]{:S(2)}, u32[]{:S(2)}) collective-permute-start(bf16[128,2048]{1,0:T(8,128)(2,1)S(1)} %slice.521), channel_id=1, source_target_pairs={{0,4},{1,5},{2,6},{3,7},{8,12},{9,13},{10,14},{11,15},{16,20},{17,... | collective-permute-start | bytes 1572872 | tf_op jit(solution)/shard_map/ppermute | solution.py:18
  830.9 45.7 %collective-permute-start.20 = (bf16[128,2048]{1,0:T(8,128)(2,1)S(1)}, bf16[128,2048]{1,0:T(8,128)(2,1)}, u32[]{:S(2)}, u32[]{:S(2)}) collective-permute-start(bf16[128,2048]{1,0:T(8,128)(2,1)S(1)} %slice.521), channel_id=1, source_target_pairs={{0,1},{1,2},{2,3},{3,4},{4,5},{5,6},{6,7},{8,9},{9,10},{10,11},{11... | collective-permute-start | bytes 1572872 | tf_op jit(solution)/shard_map/ppermute | solution.py:18
  833.8 117.8 %collective-permute-start.25 = (bf16[128,2048]{0,1:T(8,128)(2,1)}, bf16[128,2048]{0,1:T(8,128)(2,1)S(1)}, u32[]{:S(2)}, u32[]{:S(2)}) collective-permute-start(bf16[128,2048]{0,1:T(8,128)(2,1)} %bitcast.37), channel_id=1, source_target_pairs={{0,3},{1,4},{2,5},{3,6},{4,7},{8,11},{9,12},{10,13},{11,14},{12,15... | collective-permute-start | bytes 1572872 | tf_op jit(solution)/shard_map/ppermute | solution.py:18
  856.8 92.7 %collective-permute-start.24 = (bf16[128,2048]{0,1:T(8,128)(2,1)}, bf16[128,2048]{0,1:T(8,128)(2,1)S(1)}, u32[]{:S(2)}, u32[]{:S(2)}) collective-permute-start(bf16[128,2048]{0,1:T(8,128)(2,1)} %bitcast.37), channel_id=1, source_target_pairs={{0,4},{1,5},{2,6},{3,7},{8,12},{9,13},{10,14},{11,15},{16,20},{17,... | collective-permute-start | bytes 1572872 | tf_op jit(solution)/shard_map/ppermute | solution.py:18
  869.5 76.9 %collective-permute-start.23 = (bf16[128,2048]{0,1:T(8,128)(2,1)}, bf16[128,2048]{0,1:T(8,128)(2,1)}, u32[]{:S(2)}, u32[]{:S(2)}) collective-permute-start(bf16[128,2048]{0,1:T(8,128)(2,1)} %bitcast.37), channel_id=1, source_target_pairs={{0,5},{1,6},{2,7},{8,13},{9,14},{10,15},{16,21},{17,22},{18,23},{2... | collective-permute-start | bytes 1572872 | tf_op jit(solution)/shard_map/ppermute | solution.py:18
  873.5 59.6 %collective-permute-start.22 = (bf16[128,2048]{0,1:T(8,128)(2,1)}, bf16[128,2048]{0,1:T(8,128)(2,1)S(1)}, u32[]{:S(2)}, u32[]{:S(2)}) collective-permute-start(bf16[128,2048]{0,1:T(8,128)(2,1)} %bitcast.37), channel_id=1, source_target_pairs={{0,6},{1,7},{8,14},{9,15},{16,22},{17,23},{24,30},{25,31}} | collective-permute-start | bytes 1572872 | tf_op jit(solution)/shard_map/ppermute | solution.py:18
  876.7 53.5 %collective-permute-start.21 = (bf16[128,2048]{0,1:T(8,128)(2,1)}, bf16[128,2048]{0,1:T(8,128)(2,1)S(1)}, u32[]{:S(2)}, u32[]{:S(2)}) collective-permute-start(bf16[128,2048]{0,1:T(8,128)(2,1)} %bitcast.37), channel_id=1, source_target_pairs={{0,7},{8,15},{16,23},{24,31}} | collective-permute-start | bytes 1572872 | tf_op jit(solution)/shard_map/ppermute | solution.py:18
  930.2 23.6 collective-permute-start.26
  933.1 23.8 collective-permute-start.27
  946.3 108.2 %collective-permute-start.34 = (bf16[128,2048]{0,1:T(8,128)(2,1)}, bf16[128,2048]{0,1:T(8,128)(2,1)}, u32[]{:S(2)}, u32[]{:S(2)}) collective-permute-start(bf16[128,2048]{0,1:T(8,128)(2,1)} %bitcast.71), channel_id=1, source_target_pairs={{7,0},{15,8},{23,16},{31,24}} | collective-permute-start | bytes 1572872 | tf_op jit(solution)/shard_map/ppermute | solution.py:18
  949.5 106.5 %collective-permute-start.28 = (bf16[128,2048]{0,1:T(8,128)(2,1)}, bf16[128,2048]{0,1:T(8,128)(2,1)}, u32[]{:S(2)}, u32[]{:S(2)}) collective-permute-start(bf16[128,2048]{0,1:T(8,128)(2,1)} %bitcast.65), channel_id=1, source_target_pairs={{1,0},{2,1},{3,2},{4,3},{5,4},{6,5},{7,6},{9,8},{10,9},{11,10},{12... | collective-permute-start | bytes 1572872 | tf_op jit(solution)/shard_map/ppermute | solution.py:18
  951.6 106.6 %collective-permute-start.33 = (bf16[128,2048]{0,1:T(8,128)(2,1)}, bf16[128,2048]{0,1:T(8,128)(2,1)}, u32[]{:S(2)}, u32[]{:S(2)}) collective-permute-start(bf16[128,2048]{0,1:T(8,128)(2,1)} %bitcast.70), channel_id=1, source_target_pairs={{6,0},{7,1},{14,8},{15,9},{22,16},{23,17},{30,24},{31,25}} | collective-permute-start | bytes 1572872 | tf_op jit(solution)/shard_map/ppermute | solution.py:18
  953.7 105.8 %collective-permute-start.32 = (bf16[128,2048]{0,1:T(8,128)(2,1)}, bf16[128,2048]{0,1:T(8,128)(2,1)}, u32[]{:S(2)}, u32[]{:S(2)}) collective-permute-start(bf16[128,2048]{0,1:T(8,128)(2,1)} %bitcast.69), channel_id=1, source_target_pairs={{5,0},{6,1},{7,2},{13,8},{14,9},{15,10},{21,16},{22,17},{23,18},{2... | collective-permute-start | bytes 1572872 | tf_op jit(solution)/shard_map/ppermute | solution.py:18
  956.9 104.0 %collective-permute-start.31 = (bf16[128,2048]{0,1:T(8,128)(2,1)}, bf16[128,2048]{0,1:T(8,128)(2,1)}, u32[]{:S(2)}, u32[]{:S(2)}) collective-permute-start(bf16[128,2048]{0,1:T(8,128)(2,1)} %bitcast.68), channel_id=1, source_target_pairs={{4,0},{5,1},{6,2},{7,3},{12,8},{13,9},{14,10},{15,11},{20,16},{21,... | collective-permute-start | bytes 1572872 | tf_op jit(solution)/shard_map/ppermute | solution.py:18
  1056.0 17.4 collective-permute-start.29
  1058.3 39.5 %collective-permute-start.48 = (bf16[128,2048]{0,1:T(8,128)(2,1)S(1)}, bf16[128,2048]{0,1:T(8,128)(2,1)S(1)}, u32[]{:S(2)}, u32[]{:S(2)}) collective-permute-start(bf16[128,2048]{0,1:T(8,128)(2,1)S(1)} %bitcast.361), channel_id=1, source_target_pairs={{7,0},{15,8},{23,16},{31,24}} | collective-permute-start | bytes 1572872 | tf_op jit(solution)/shard_map/ppermute | solution.py:18
  1059.6 39.5 %collective-permute-start.42 = (bf16[128,2048]{0,1:T(8,128)(2,1)S(1)}, bf16[128,2048]{0,1:T(8,128)(2,1)S(1)}, u32[]{:S(2)}, u32[]{:S(2)}) collective-permute-start(bf16[128,2048]{0,1:T(8,128)(2,1)S(1)} %bitcast.360), channel_id=1, source_target_pairs={{1,0},{2,1},{3,2},{4,3},{5,4},{6,5},{7,6},{9,8},{10,9},{11,10},{12... | collective-permute-start | bytes 1572872 | tf_op jit(solution)/shard_map/ppermute | solution.py:18
  1060.9 39.9 %collective-permute-start.47 = (bf16[128,2048]{0,1:T(8,128)(2,1)S(1)}, bf16[128,2048]{0,1:T(8,128)(2,1)S(1)}, u32[]{:S(2)}, u32[]{:S(2)}) collective-permute-start(bf16[128,2048]{0,1:T(8,128)(2,1)S(1)} %bitcast.359), channel_id=1, source_target_pairs={{6,0},{7,1},{14,8},{15,9},{22,16},{23,17},{30,24},{31,25}} | collective-permute-start | bytes 1572872 | tf_op jit(solution)/shard_map/ppermute | solution.py:18
  1068.1 33.9 %collective-permute-start.46 = (bf16[128,2048]{0,1:T(8,128)(2,1)S(1)}, bf16[128,2048]{0,1:T(8,128)(2,1)S(1)}, u32[]{:S(2)}, u32[]{:S(2)}) collective-permute-start(bf16[128,2048]{0,1:T(8,128)(2,1)S(1)} %bitcast.358), channel_id=1, source_target_pairs={{5,0},{6,1},{7,2},{13,8},{14,9},{15,10},{21,16},{22,17},{23,18},{2... | collective-permute-start | bytes 1572872 | tf_op jit(solution)/shard_map/ppermute | solution.py:18
  1073.4 30.0 %collective-permute-start.45 = (bf16[128,2048]{0,1:T(8,128)(2,1)S(1)}, bf16[128,2048]{0,1:T(8,128)(2,1)S(1)}, u32[]{:S(2)}, u32[]{:S(2)}) collective-permute-start(bf16[128,2048]{0,1:T(8,128)(2,1)S(1)} %bitcast.357), channel_id=1, source_target_pairs={{4,0},{5,1},{6,2},{7,3},{12,8},{13,9},{14,10},{15,11},{20,16},{21,... | collective-permute-start | bytes 1572872 | tf_op jit(solution)/shard_map/ppermute | solution.py:18
  1097.8 23.6 collective-permute-start.44
  1099.1 23.6 collective-permute-start.43
  1100.8 47.6 %collective-permute-start.41 = (bf16[128,2048]{0,1:T(8,128)(2,1)S(1)}, bf16[128,2048]{0,1:T(8,128)(2,1)S(1)}, u32[]{:S(2)}, u32[]{:S(2)}) collective-permute-start(bf16[128,2048]{0,1:T(8,128)(2,1)S(1)} %bitcast.354), channel_id=1, source_target_pairs={{7,0},{15,8},{23,16},{31,24}} | collective-permute-start | bytes 1572872 | tf_op jit(solution)/shard_map/ppermute | solution.py:18
  1102.1 47.5 %collective-permute-start.35 = (bf16[128,2048]{0,1:T(8,128)(2,1)S(1)}, bf16[128,2048]{0,1:T(8,128)(2,1)S(1)}, u32[]{:S(2)}, u32[]{:S(2)}) collective-permute-start(bf16[128,2048]{0,1:T(8,128)(2,1)S(1)} %bitcast.353), channel_id=1, source_target_pairs={{1,0},{2,1},{3,2},{4,3},{5,4},{6,5},{7,6},{9,8},{10,9},{11,10},{12... | collective-permute-start | bytes 1572872 | tf_op jit(solution)/shard_map/ppermute | solution.py:18
  1103.4 48.8 %collective-permute-start.40 = (bf16[128,2048]{0,1:T(8,128)(2,1)S(1)}, bf16[128,2048]{0,1:T(8,128)(2,1)S(1)}, u32[]{:S(2)}, u32[]{:S(2)}) collective-permute-start(bf16[128,2048]{0,1:T(8,128)(2,1)S(1)} %bitcast.351), channel_id=1, source_target_pairs={{6,0},{7,1},{14,8},{15,9},{22,16},{23,17},{30,24},{31,25}} | collective-permute-start | bytes 1572872 | tf_op jit(solution)/shard_map/ppermute | solution.py:18
  1121.4 32.1 %collective-permute-start.39 = (bf16[128,2048]{0,1:T(8,128)(2,1)S(1)}, bf16[128,2048]{0,1:T(8,128)(2,1)S(1)}, u32[]{:S(2)}, u32[]{:S(2)}) collective-permute-start(bf16[128,2048]{0,1:T(8,128)(2,1)S(1)} %bitcast.349), channel_id=1, source_target_pairs={{5,0},{6,1},{7,2},{13,8},{14,9},{15,10},{21,16},{22,17},{23,18},{2... | collective-permute-start | bytes 1572872 | tf_op jit(solution)/shard_map/ppermute | solution.py:18
  1122.7 37.2 %collective-permute-start.38 = (bf16[128,2048]{0,1:T(8,128)(2,1)S(1)}, bf16[128,2048]{0,1:T(8,128)(2,1)S(1)}, u32[]{:S(2)}, u32[]{:S(2)}) collective-permute-start(bf16[128,2048]{0,1:T(8,128)(2,1)S(1)} %bitcast.348), channel_id=1, source_target_pairs={{4,0},{5,1},{6,2},{7,3},{12,8},{13,9},{14,10},{15,11},{20,16},{21,... | collective-permute-start | bytes 1572872 | tf_op jit(solution)/shard_map/ppermute | solution.py:18
  1149.6 16.8 collective-permute-start.36
  1152.2 41.1 %collective-permute-start.55 = (bf16[128,2048]{0,1:T(8,128)(2,1)S(1)}, bf16[128,2048]{0,1:T(8,128)(2,1)S(1)}, u32[]{:S(2)}, u32[]{:S(2)}) collective-permute-start(bf16[128,2048]{0,1:T(8,128)(2,1)S(1)} %bitcast.345), channel_id=1, source_target_pairs={{7,0},{15,8},{23,16},{31,24}} | collective-permute-start | bytes 1572872 | tf_op jit(solution)/shard_map/ppermute | solution.py:18
  1153.5 41.1 %collective-permute-start.49 = (bf16[128,2048]{0,1:T(8,128)(2,1)S(1)}, bf16[128,2048]{0,1:T(8,128)(2,1)S(1)}, u32[]{:S(2)}, u32[]{:S(2)}) collective-permute-start(bf16[128,2048]{0,1:T(8,128)(2,1)S(1)} %bitcast.344), channel_id=1, source_target_pairs={{1,0},{2,1},{3,2},{4,3},{5,4},{6,5},{7,6},{9,8},{10,9},{11,10},{12... | collective-permute-start | bytes 1572872 | tf_op jit(solution)/shard_map/ppermute | solution.py:18
  1159.9 37.3 %collective-permute-start.54 = (bf16[128,2048]{0,1:T(8,128)(2,1)S(1)}, bf16[128,2048]{0,1:T(8,128)(2,1)S(1)}, u32[]{:S(2)}, u32[]{:S(2)}) collective-permute-start(bf16[128,2048]{0,1:T(8,128)(2,1)S(1)} %bitcast.343), channel_id=1, source_target_pairs={{6,0},{7,1},{14,8},{15,9},{22,16},{23,17},{30,24},{31,25}} | collective-permute-start | bytes 1572872 | tf_op jit(solution)/shard_map/ppermute | solution.py:18
  1162.5 34.7 %collective-permute-start.53 = (bf16[128,2048]{0,1:T(8,128)(2,1)S(1)}, bf16[128,2048]{0,1:T(8,128)(2,1)S(1)}, u32[]{:S(2)}, u32[]{:S(2)}) collective-permute-start(bf16[128,2048]{0,1:T(8,128)(2,1)S(1)} %bitcast.342), channel_id=1, source_target_pairs={{5,0},{6,1},{7,2},{13,8},{14,9},{15,10},{21,16},{22,17},{23,18},{2... | collective-permute-start | bytes 1572872 | tf_op jit(solution)/shard_map/ppermute | solution.py:18
  1166.4 44.4 %collective-permute-start.52 = (bf16[128,2048]{0,1:T(8,128)(2,1)S(1)}, bf16[128,2048]{0,1:T(8,128)(2,1)S(1)}, u32[]{:S(2)}, u32[]{:S(2)}) collective-permute-start(bf16[128,2048]{0,1:T(8,128)(2,1)S(1)} %bitcast.341), channel_id=1, source_target_pairs={{4,0},{5,1},{6,2},{7,3},{12,8},{13,9},{14,10},{15,11},{20,16},{21,... | collective-permute-start | bytes 1572872 | tf_op jit(solution)/shard_map/ppermute | solution.py:18
  1193.3 17.5 collective-permute-start.51
  1194.7 16.9 collective-permute-start.50
  1413.9 44.1 %all-to-all-start.1 = ((bf16[2,8,16,2048]{3,2,0,1:T(8,128)(2,1)}), bf16[2,8,16,2048]{3,2,0,1:T(8,128)(2,1)}, u32[]{:S(2)}, u32[]{:S(2)}) async-start(bf16[2,8,16,2048]{3,2,0,1:T(8,128)(2,1)} %pad_maximum_fusion.3), calls=%async_computation.1 | async-start | bytes 2097152 | tf_op jit(solution)/shard_map/all_to_all | solution.py:338
  1458.0 55.2 %all-to-all-start.3 = ((bf16[2,8,16,2048]{3,2,0,1:T(8,128)(2,1)}), bf16[2,8,16,2048]{3,2,0,1:T(8,128)(2,1)S(1)}, u32[]{:S(2)}, u32[]{:S(2)}) async-start(bf16[2,8,16,2048]{3,2,0,1:T(8,128)(2,1)} %pad_maximum_fusion.4), calls=%async_computation.3 | async-start | bytes 2097152 | tf_op jit(solution)/shard_map/all_to_all | solution.py:339
  (134 other events, 6054.0 us)
Sparse Core Ops, SparseCore 0:
  9.9 66.3 all-gather.11
  78.2 136.8 all-gather.9
  217.0 160.7 all-gather.15
  379.5 160.7 all-gather.13
  593.9 311.7 reduce-scatter.4
  1287.9 418.0 reduce-scatter.2
where the time goes:
time: 2580 us; the launch traced here: 2570 us
  blocking collectives  963 us (37%)
  waiting for transfers between devices  826 us (32%)
  matrix products  385 us (15%)
  local copies, waits for them, and re-layouts  135 us (5%)
  starting transfers between devices  134 us (5%)
  other arithmetic  106 us (4%)
    psum x1, blocking collectives, reduce_grads(): lax.psum((wide, deep, scattered[0], scattered[1], scattered[2], scattered...  840 us
    ppermute x56, waiting for transfers between devices, shifted(): return lax.ppermute(block, axis, route)  275 us
    reduce_scatter x1, waiting for transfers between devices, reduce_grads(): lax.psum_scatter(jnp.concatenate([contract_first(hn_rows, dqkv_rows), con...  187 us
    all_gather x1, waiting for transfers between devices, body(): lax.all_gather(shards[8], 'shard', axis=0, tiled=True)  148 us
    dot_general x8, matrix products, contract_last(): lax.dot_general(left, right, (((1,), (1,)), ((), ())), preferred_element_...  129 us
    all_gather x1, waiting for transfers between devices, body(): lax.all_gather(shards[6], 'shard', axis=0, tiled=True)  125 us
    ppermute x56, starting transfers between devices, shifted(): return lax.ppermute(block, axis, route)  106 us
    all_gather x1, waiting for transfers between devices, body(): lax.all_gather(shards[2], 'shard', axis=0, tiled=True)  74.5 us
  transfers between devices with their start and end apart: 66, of which 22 were waited for; matrix products, arithmetic and copies ran while one was open for 21% of the time, Pallas kernels for 0%

commit v1 on v0

--- a/solution.py
+++ b/solution.py
@@ -10,6 +10,22 @@
 BLOCK = 128
 MICRO = 2
 MAXBLK = 8
+
+
+def collect(x, axis, dim):
+    ways, here, step = (lax.axis_size(axis), lax.axis_index(axis), x.shape[dim])
+    lengths = [n * ways if d == dim else n for d, n in enumerate(x.shape)]
+    full = lax.dynamic_update_slice_in_dim(jnp.zeros(lengths, x.dtype), x, here * step, axis=dim)
+    going_up = going_down = x
+    for far in range(1, ways // 2 + 1):
+        going_up = lax.ppermute(going_up, axis, [(d, (d + 1) % ways) for d in range(ways)])
+        full = lax.dynamic_update_slice_in_dim(full, going_up, (here - far) % ways * step, axis=dim)
+        if 2 * far < ways:
+            going_down = lax.ppermute(going_down, axis, [(d, (d - 1) % ways) for d in range(ways)])
+            full = lax.dynamic_update_slice_in_dim(
+                full, going_down, (here + far) % ways * step, axis=dim
+            )
+    return full
 
 
 def shifted(block, axis, distance):
@@ -182,7 +198,7 @@
         lax.all_gather(shards[3], "shard", axis=0, tiled=True),
         lax.all_gather(shards[4], "shard", axis=0, tiled=True),
         lax.all_gather(shards[5], "shard", axis=0, tiled=True),
-        lax.all_gather(shards[6], "shard", axis=0, tiled=True),
+        collect(shards[6], "shard", 0),
         lax.all_gather(shards[7], "shard", axis=0, tiled=True),
         lax.all_gather(shards[8], "shard", axis=0, tiled=True),
         lax.all_gather(shards[9], "shard", axis=0, tiled=True),

time: 2580 us -> 2720 us (1.054)
  blocking collectives: 963 us -> 1110 us
  waiting for transfers between devices: 826 us -> 777 us
  local copies, waits for them, and re-layouts: 135 us -> 179 us
    ppermute x0 -> x7, waiting for transfers between devices: none -> 294 us  [the longest x4 292 us: collect(): lax.ppermute(going_up, axis, [(d, (d + 1) % ways) for d in range(ways)])]
    all_gather x1, blocking collectives: 24.7 us -> 177 us  [body(): lax.all_gather(shards[1], 'shard', axis=0, tiled=True)]
    all_gather x1, waiting for transfers between devices: 148 us -> 0.02 us  [body(): lax.all_gather(shards[8], 'shard', axis=0, tiled=True)]
    all_gather x1 -> x0, waiting for transfers between devices: 125 us -> none  [body(): lax.all_gather(shards[6], 'shard', axis=0, tiled=True)]
    all_gather x1, waiting for transfers between devices: 74.5 us -> 0.01 us  [body(): lax.all_gather(shards[2], 'shard', axis=0, tiled=True)]
    dynamic_update_slice x0 -> x8, local copies, waits for them, and re-layouts: none -> 32.7 us  [the longest x4 18.9 us: collect(): lax.dynamic_update_slice_in_dim(full, going_up, (here - far) % ways * ste...]
  transfers between devices with their start and end apart: 66 -> 72, of which waited for: 22 -> 23; matrix products, arithmetic and copies ran while one was open for 21% -> 20% of each run, Pallas kernels for 0% -> 0%
where the time goes in v1:
time: 2720 us; the launch traced here: 2710 us
  blocking collectives  1110 us (41%)
  waiting for transfers between devices  777 us (29%)
  matrix products  378 us (14%)
  local copies, waits for them, and re-layouts  179 us (7%)
  starting transfers between devices  132 us (5%)
  other arithmetic  107 us (4%)
    psum x1, blocking collectives, reduce_grads(): lax.psum((wide, deep, scattered[0], scattered[1], scattered[2], scattered...  839 us
    ppermute x4, waiting for transfers between devices, collect(): lax.ppermute(going_up, axis, [(d, (d + 1) % ways) for d in range(ways)])  292 us
    ppermute x56, waiting for transfers between devices, shifted(): return lax.ppermute(block, axis, route)  269 us
    reduce_scatter x1, waiting for transfers between devices, reduce_grads(): lax.psum_scatter(jnp.concatenate([contract_first(hn_rows, dqkv_rows), con...  192 us
    all_gather x1, blocking collectives, body(): lax.all_gather(shards[1], 'shard', axis=0, tiled=True)  177 us
    dot_general x8, matrix products, contract_last(): lax.dot_general(left, right, (((1,), (1,)), ((), ())), preferred_element_...  127 us
    ppermute x56, starting transfers between devices, shifted(): return lax.ppermute(block, axis, route)  105 us
  transfers between devices with their start and end apart: 72, of which 23 were waited for; matrix products, arithmetic and copies ran while one was open for 20% of the time, Pallas kernels for 0%

profile of v1, /device:TPU:0, one launch (start us, length us, event | category | flops | bytes accessed | tf_op | source)
XLA Modules:
  0.0 2706.9 jit_solution(17629179283110796931)
XLA Ops:
  13.5 11.4 scatter_fusion
  39.6 114.9 %collective-permute-done.14 = bf16[256,8192]{1,0:T(8,128)(2,1)} collective-permute-done((bf16[256,8192]{1,0:T(8,128)(2,1)}, bf16[256,8192]{1,0:T(8,128)(2,1)}, u32[]{:S(2)}, u32[]{:S(2)}) %collective-permute-start.14) | collective-permute-done | bytes 4194336 | tf_op jit(solution)/shard_map/ppermute | solution.py:21
  165.7 176.9 %all-gather.1 = bf16[8,1,256]{2,1,0:T(2,128)(2,1)S(1)} all-gather(bf16[1,1,256]{2,1,0:T(2,128)(2,1)S(1)} %reshape.784), channel_id=1, replica_groups=mesh['rep'=4,'shard'=8] {'shard'}, dimensions={0}, use_global_device_ids=true | all-gather | bytes 4608 | tf_op jit(solution)/shard_map/all_gather | solution.py:196
  342.7 8.9 all-gather
  351.7 7.9 all_gather.33
  359.6 9.6 all-gather.2
  370.2 11.7 broadcast_in_dim.237
  389.8 19.8 all-to-all-done.2
  412.1 4.9 constant_dynamic-update-slice_fusion.38
  421.7 159.2 %collective-permute-done.18 = bf16[256,8192]{1,0:T(8,128)(2,1)} collective-permute-done((bf16[256,8192]{1,0:T(8,128)(2,1)}, bf16[256,8192]{1,0:T(8,128)(2,1)}, u32[]{:S(2)}, u32[]{:S(2)}) %collective-permute-start.18) | collective-permute-done | bytes 4194336 | tf_op jit(solution)/shard_map/ppermute | solution.py:21
  597.1 6.3 convolution_convert_fusion.5
  604.4 6.3 convolution_convert_fusion.4
  611.7 18.3 collective-permute-done.20
  634.6 10.2 convolution_add_fusion.3
  649.5 17.4 fusion.171
  667.0 18.5 convert_reduce_fusion.1
  685.5 17.4 fusion.172
  702.9 18.7 convert_reduce_fusion
  721.6 16.1 convolution_convert_fusion
  752.4 14.5 convolution_add_fusion.2
  782.7 5.8 collective-permute-start.5
  810.0 65.2 %collective-permute-done = bf16[128,2048]{1,0:T(8,128)(2,1)S(1)} collective-permute-done((bf16[128,2048]{1,0:T(8,128)(2,1)S(1)}, bf16[128,2048]{1,0:T(8,128)(2,1)S(1)}, u32[]{:S(2)}, u32[]{:S(2)}) %collective-permute-start) | collective-permute-done | bytes 524320 | tf_op jit(solution)/shard_map/ppermute | solution.py:34
  879.5 7.4 collective-permute-start.26
  887.8 17.4 collective-permute-done.3
  916.6 56.5 %collective-permute-done.21 = bf16[128,2048]{1,0:T(8,128)(2,1)S(1)} collective-permute-done((bf16[128,2048]{1,0:T(8,128)(2,1)S(1)}, bf16[128,2048]{1,0:T(8,128)(2,1)S(1)}, u32[]{:S(2)}, u32[]{:S(2)}) %collective-permute-start.21) | collective-permute-done | bytes 524320 | tf_op jit(solution)/shard_map/ppermute | solution.py:34
  978.3 5.5 collective-permute-start.32
  984.6 8.8 collective-permute-done.24
  993.4 5.3 collective-permute-start.31
  999.5 6.5 copy.93
  1017.9 13.8 multiply_reduce_fusion.1
  1031.7 13.6 multiply_convert_fusion.1
  1053.5 10.4 fusion.167
  1074.0 6.4 copy.96
  1109.6 9.1 fusion.169
  1119.8 13.7 multiply_reduce_fusion
  1133.5 13.9 multiply_convert_fusion
  1153.3 5.3 fusion.64
  1159.7 7.8 fusion.63
  1167.7 6.7 fusion.66
  1174.4 9.8 fusion.65
  1184.2 5.7 convolution_convert_fusion.3
  1201.1 6.1 collective-permute-done.37
  1215.8 20.8 collective-permute-done.55
  1243.5 16.6 collective-permute-done.51
  1263.5 23.6 collective-permute-done.48
  1306.4 25.6 collective-permute-done.62
  1335.9 13.6 collective-permute-done.59
  1350.9 15.1 convolution_convert_fusion.2
  1366.1 15.6 convolution_convert_fusion.1
  1381.6 44.7 %pad_maximum_fusion = bf16[2048,16384]{1,0:T(8,128)(2,1)} fusion(bf16[2048,2048]{1,0:T(8,128)(2,1)} %convolution_convert_fusion.3, bf16[2048,8192]{1,0:T(8,128)(2,1)} %convolution_convert_fusion.1, bf16[2048,6144]{1,0:T(8,128)(2,1)} %convolution_convert_fusion.2), kind=kLoop, calls=%fused_computation.5 | loop fusion | flops 201326592 | bytes 134217728 | tf_op jit(solution)/shard_map/concatenate | solution.py:100
  1429.8 17.5 all-gather.4
  1447.3 9.6 all-gather.3
  1460.5 7.3 convolution_add_fusion.9
  1467.8 7.4 convolution_add_fusion.8
  1476.2 19.0 fusion.97
  1495.2 18.5 fusion.96
  1513.8 22.3 convolution_add_fusion.4
  1536.1 20.1 multiply_reduce_fusion.3
  1563.1 14.5 fusion.62
  1577.7 13.9 fusion.61
  1596.8 45.2 %all-reduce.22 = (bf16[2048]{0:T(1024)(128)(2,1)S(1)}, bf16[2048]{0:T(1024)(128)(2,1)S(1)}, bf16[6144]{0:T(1024)(128)(2,1)S(1)}, bf16[2048]{0:T(1024)(128)(2,1)S(1)}, bf16[8192]{0:T(1024)(128)(2,1)S(1)}) all-reduce(bf16[2048]{0:T(1024)(128)(2,1)S(1)} %add_convert_fusion.12, ...), channel_id=2, replica_groups=mesh['rep'=4,'shard'=8] {'shard'}, use_global_device_ids=true, to_apply=%region_25.27.clone | all-reduce | flops 20480 | bytes 81920
  1654.0 192.0 %reduce-scatter.3.cloned.1.call-done = bf16[256,16384]{1,0:T(8,128)(2,1)} async-done(((bf16[2048,16384]{1,0:T(8,128)(2,1)}), bf16[256,16384]{1,0:T(8,128)(2,1)}) %reduce-scatter.3.cloned.1.call-update) | async-done | bytes 8388624 | tf_op jit(solution)/shard_map/reduce_scatter | solution.py:99
  1846.0 839.4 %all-reduce.24 = (f32[256]{0:T(256)}, f32[256]{0:T(256)}, f32[256,16384]{1,0:T(8,128)}, f32[768]{0:T(1024)}, f32[256]{0:T(256)S(1)}, /*index=5*/f32[1024]{0:T(1024)}, f32[1024,2048]{1,0:T(8,128)}) all-reduce(f32[256]{0:T(256)S(1)} %dynamic-slice_convert_fusion.4, ...), channel_id=1, replica_groups=mesh['rep'=4,'shard'=8] {'rep'}, use_global_device_ids=true, to_apply=%region_26.28 | all-reduce | flops 6294016 | bytes 37769216 | tf_op jit(solution)/shard_map/psum | solution.py:135
  2688.6 6.9 slice.442
  (588 shorter events, 309.4 us)
Async XLA Ops:
  7.2 589.9 %all-gather.11.cloned.1.call-start = ((), (), s32[]{:S(2)}) async-start(), calls=%async_computation.7 | async-start | bytes 9437184 | tf_op jit(solution)/shard_map/all_gather | solution.py:199
  7.9 626.7 %all-gather.9.cloned.1.call-start = ((), (), s32[]{:S(2)}) async-start(), calls=%async_computation.6 | async-start | bytes 28311552 | tf_op jit(solution)/shard_map/all_gather | solution.py:197
  8.7 640.8 %all-gather.13.cloned.1.call-start = ((), (), s32[]{:S(2)}) async-start(), calls=%async_computation.8 | async-start | bytes 37748736 | tf_op jit(solution)/shard_map/all_gather | solution.py:203
  9.4 145.0 %collective-permute-start.14 = (bf16[256,8192]{1,0:T(8,128)(2,1)}, bf16[256,8192]{1,0:T(8,128)(2,1)}, u32[]{:S(2)}, u32[]{:S(2)}) collective-permute-start(bf16[256,8192]{1,0:T(8,128)(2,1)} %param.26), channel_id=1, source_target_pairs={{0,1},{1,2},{2,3},{3,4},{4,5},{5,6},{6,7},{7,0},{8,9},{9,10},{10,1... | collective-permute-start | bytes 12582920 | tf_op jit(solution)/shard_map/ppermute | solution.py:21
  9.9 152.7 %collective-permute-start.15 = (bf16[256,8192]{1,0:T(8,128)(2,1)}, bf16[256,8192]{1,0:T(8,128)(2,1)}, u32[]{:S(2)}, u32[]{:S(2)}) collective-permute-start(bf16[256,8192]{1,0:T(8,128)(2,1)} %param.26), channel_id=1, source_target_pairs={{0,7},{1,0},{2,1},{3,2},{4,3},{5,4},{6,5},{7,6},{8,15},{9,8},{10,9... | collective-permute-start | bytes 12582920 | tf_op jit(solution)/shard_map/ppermute | solution.py:24
  35.5 348.7 %all-to-all-start = ((bf16[2,8,16,2048]{3,2,0,1:T(8,128)(2,1)}), bf16[2,8,16,2048]{3,2,0,1:T(8,128)(2,1)S(1)}, u32[]{:S(2)}, u32[]{:S(2)}) async-start(bf16[2,8,16,2048]{3,2,0,1:T(8,128)(2,1)} %copy.92), calls=%async_computation | async-start | bytes 2097152 | tf_op jit(solution)/shard_map/all_to_all | solution.py:177
  154.4 234.0 %collective-permute-start.16 = (bf16[256,8192]{1,0:T(8,128)(2,1)}, bf16[256,8192]{1,0:T(8,128)(2,1)}, u32[]{:S(2)}, u32[]{:S(2)}) collective-permute-start(bf16[256,8192]{1,0:T(8,128)(2,1)} %collective-permute-done.14), channel_id=1, source_target_pairs={{0,1},{1,2},{2,3},{3,4},{4,5},{5,6},{6,7},{7,0},{8,9},{9,10},{10,1... | collective-permute-start | bytes 12582920 | tf_op jit(solution)/shard_map/ppermute | solution.py:21
  162.6 249.4 %collective-permute-start.17 = (bf16[256,8192]{1,0:T(8,128)(2,1)}, bf16[256,8192]{1,0:T(8,128)(2,1)}, u32[]{:S(2)}, u32[]{:S(2)}) collective-permute-start(bf16[256,8192]{1,0:T(8,128)(2,1)} %collective-permute-done.15), channel_id=1, source_target_pairs={{0,7},{1,0},{2,1},{3,2},{4,3},{5,4},{6,5},{7,6},{8,15},{9,8},{10,9... | collective-permute-start | bytes 12582920 | tf_op jit(solution)/shard_map/ppermute | solution.py:24
  384.2 25.3 all-to-all-start.2
  387.7 1266.2 %reduce-scatter.5.cloned.1.call-start = ((), (), s32[]{:S(2)}) async-start(), calls=%async_computation.10 | async-start | bytes 37748736 | tf_op jit(solution)/shard_map/reduce_scatter | solution.py:112
  388.4 192.5 %collective-permute-start.18 = (bf16[256,8192]{1,0:T(8,128)(2,1)}, bf16[256,8192]{1,0:T(8,128)(2,1)}, u32[]{:S(2)}, u32[]{:S(2)}) collective-permute-start(bf16[256,8192]{1,0:T(8,128)(2,1)} %collective-permute-done.16), channel_id=1, source_target_pairs={{0,1},{1,2},{2,3},{3,4},{4,5},{5,6},{6,7},{7,0},{8,9},{9,10},{10,1... | collective-permute-start | bytes 12582920 | tf_op jit(solution)/shard_map/ppermute | solution.py:21
  412.0 182.9 %collective-permute-start.19 = (bf16[256,8192]{1,0:T(8,128)(2,1)}, bf16[256,8192]{1,0:T(8,128)(2,1)S(1)}, u32[]{:S(2)}, u32[]{:S(2)}) collective-permute-start(bf16[256,8192]{1,0:T(8,128)(2,1)} %collective-permute-done.17), channel_id=1, source_target_pairs={{0,7},{1,0},{2,1},{3,2},{4,3},{5,4},{6,5},{7,6},{8,15},{9,8},{10,9... | collective-permute-start | bytes 12582920 | tf_op jit(solution)/shard_map/ppermute | solution.py:24
  580.9 49.1 %collective-permute-start.20 = (bf16[256,8192]{1,0:T(8,128)(2,1)}, bf16[256,8192]{1,0:T(8,128)(2,1)}, u32[]{:S(2)}, u32[]{:S(2)}) collective-permute-start(bf16[256,8192]{1,0:T(8,128)(2,1)} %collective-permute-done.18), channel_id=1, source_target_pairs={{0,1},{1,2},{2,3},{3,4},{4,5},{5,6},{6,7},{7,0},{8,9},{9,10},{10,1... | collective-permute-start | bytes 12582920 | tf_op jit(solution)/shard_map/ppermute | solution.py:21
  737.7 1108.2 %reduce-scatter.3.cloned.1.call-start = ((), (), s32[]{:S(2)}) async-start(), calls=%async_computation.9 | async-start | bytes 75497472 | tf_op jit(solution)/shard_map/reduce_scatter | solution.py:99
  738.9 53.4 %collective-permute-start.11 = (bf16[128,2048]{0,1:T(8,128)(2,1)}, bf16[128,2048]{0,1:T(8,128)(2,1)}, u32[]{:S(2)}, u32[]{:S(2)}) collective-permute-start(bf16[128,2048]{0,1:T(8,128)(2,1)} %bitcast.18), channel_id=1, source_target_pairs={{0,3},{1,4},{2,5},{3,6},{4,7},{8,11},{9,12},{10,13},{11,14},{12,15... | collective-permute-start | bytes 1572872 | tf_op jit(solution)/shard_map/ppermute | solution.py:34
  741.0 48.7 %collective-permute-start.10 = (bf16[128,2048]{0,1:T(8,128)(2,1)}, bf16[128,2048]{0,1:T(8,128)(2,1)}, u32[]{:S(2)}, u32[]{:S(2)}) collective-permute-start(bf16[128,2048]{0,1:T(8,128)(2,1)} %bitcast.18), channel_id=1, source_target_pairs={{0,4},{1,5},{2,6},{3,7},{8,12},{9,13},{10,14},{11,15},{16,20},{17,... | collective-permute-start | bytes 1572872 | tf_op jit(solution)/shard_map/ppermute | solution.py:34
  744.3 38.4 %collective-permute-start.9 = (bf16[128,2048]{0,1:T(8,128)(2,1)}, bf16[128,2048]{0,1:T(8,128)(2,1)}, u32[]{:S(2)}, u32[]{:S(2)}) collective-permute-start(bf16[128,2048]{0,1:T(8,128)(2,1)} %bitcast.18), channel_id=1, source_target_pairs={{0,5},{1,6},{2,7},{8,13},{9,14},{10,15},{16,21},{17,22},{18,23},{2... | collective-permute-start | bytes 1572872 | tf_op jit(solution)/shard_map/ppermute | solution.py:34
  746.4 33.3 %collective-permute-start.8 = (bf16[128,2048]{0,1:T(8,128)(2,1)}, bf16[128,2048]{0,1:T(8,128)(2,1)}, u32[]{:S(2)}, u32[]{:S(2)}) collective-permute-start(bf16[128,2048]{0,1:T(8,128)(2,1)} %bitcast.18), channel_id=1, source_target_pairs={{0,6},{1,7},{8,14},{9,15},{16,22},{17,23},{24,30},{25,31}} | collective-permute-start | bytes 1572872 | tf_op jit(solution)/shard_map/ppermute | solution.py:34
  748.5 28.5 %collective-permute-start.7 = (bf16[128,2048]{0,1:T(8,128)(2,1)}, bf16[128,2048]{0,1:T(8,128)(2,1)}, u32[]{:S(2)}, u32[]{:S(2)}) collective-permute-start(bf16[128,2048]{0,1:T(8,128)(2,1)} %bitcast.18), channel_id=1, source_target_pairs={{0,7},{8,15},{16,23},{24,31}} | collective-permute-start | bytes 1572872 | tf_op jit(solution)/shard_map/ppermute | solution.py:34
  777.0 20.3 collective-permute-start.12
  782.7 127.5 %collective-permute-start.5 = (bf16[128,2048]{1,0:T(8,128)(2,1)S(1)}, bf16[128,2048]{1,0:T(8,128)(2,1)S(1)}, u32[]{:S(2)}, u32[]{:S(2)}) collective-permute-start(bf16[128,2048]{1,0:T(8,128)(2,1)S(1)} %slice.522), channel_id=1, source_target_pairs={{0,2},{1,3},{2,4},{3,5},{4,6},{5,7},{8,10},{9,11},{10,12},{11,13},... | collective-permute-start | bytes 1572872 | tf_op jit(solution)/shard_map/ppermute | solution.py:34
  789.8 118.3 %collective-permute-start.4 = (bf16[128,2048]{1,0:T(8,128)(2,1)S(1)}, bf16[128,2048]{1,0:T(8,128)(2,1)S(1)}, u32[]{:S(2)}, u32[]{:S(2)}) collective-permute-start(bf16[128,2048]{1,0:T(8,128)(2,1)S(1)} %slice.522), channel_id=1, source_target_pairs={{0,3},{1,4},{2,5},{3,6},{4,7},{8,11},{9,12},{10,13},{11,14},{12,15... | collective-permute-start | bytes 1572872 | tf_op jit(solution)/shard_map/ppermute | solution.py:34
  792.3 87.2 %collective-permute-start.2 = (bf16[128,2048]{1,0:T(8,128)(2,1)S(1)}, bf16[128,2048]{1,0:T(8,128)(2,1)S(1)}, u32[]{:S(2)}, u32[]{:S(2)}) collective-permute-start(bf16[128,2048]{1,0:T(8,128)(2,1)S(1)} %slice.522), channel_id=1, source_target_pairs={{0,5},{1,6},{2,7},{8,13},{9,14},{10,15},{16,21},{17,22},{18,23},{2... | collective-permute-start | bytes 1572872 | tf_op jit(solution)/shard_map/ppermute | solution.py:34
  797.3 80.1 %collective-permute-start.1 = (bf16[128,2048]{1,0:T(8,128)(2,1)S(1)}, bf16[128,2048]{1,0:T(8,128)(2,1)S(1)}, u32[]{:S(2)}, u32[]{:S(2)}) collective-permute-start(bf16[128,2048]{1,0:T(8,128)(2,1)S(1)} %slice.522), channel_id=1, source_target_pairs={{0,6},{1,7},{8,14},{9,15},{16,22},{17,23},{24,30},{25,31}} | collective-permute-start | bytes 1572872 | tf_op jit(solution)/shard_map/ppermute | solution.py:34
  798.8 76.4 %collective-permute-start = (bf16[128,2048]{1,0:T(8,128)(2,1)S(1)}, bf16[128,2048]{1,0:T(8,128)(2,1)S(1)}, u32[]{:S(2)}, u32[]{:S(2)}) collective-permute-start(bf16[128,2048]{1,0:T(8,128)(2,1)S(1)} %slice.522), channel_id=1, source_target_pairs={{0,7},{8,15},{16,23},{24,31}} | collective-permute-start | bytes 1572872 | tf_op jit(solution)/shard_map/ppermute | solution.py:34
  875.2 29.9 %collective-permute-start.3 = (bf16[128,2048]{1,0:T(8,128)(2,1)S(1)}, bf16[128,2048]{1,0:T(8,128)(2,1)S(1)}, u32[]{:S(2)}, u32[]{:S(2)}) collective-permute-start(bf16[128,2048]{1,0:T(8,128)(2,1)S(1)} %slice.522), channel_id=1, source_target_pairs={{0,4},{1,5},{2,6},{3,7},{8,12},{9,13},{10,14},{11,15},{16,20},{17,... | collective-permute-start | bytes 1572872 | tf_op jit(solution)/shard_map/ppermute | solution.py:34
  877.4 35.0 %collective-permute-start.6 = (bf16[128,2048]{1,0:T(8,128)(2,1)S(1)}, bf16[128,2048]{1,0:T(8,128)(2,1)S(1)}, u32[]{:S(2)}, u32[]{:S(2)}) collective-permute-start(bf16[128,2048]{1,0:T(8,128)(2,1)S(1)} %slice.522), channel_id=1, source_target_pairs={{0,1},{1,2},{2,3},{3,4},{4,5},{5,6},{6,7},{8,9},{9,10},{10,11},{11... | collective-permute-start | bytes 1572872 | tf_op jit(solution)/shard_map/ppermute | solution.py:34
  879.5 130.4 %collective-permute-start.26 = (bf16[128,2048]{1,0:T(8,128)(2,1)S(1)}, bf16[128,2048]{1,0:T(8,128)(2,1)}, u32[]{:S(2)}, u32[]{:S(2)}) collective-permute-start(bf16[128,2048]{1,0:T(8,128)(2,1)S(1)} %slice.521), channel_id=1, source_target_pairs={{0,2},{1,3},{2,4},{3,5},{4,6},{5,7},{8,10},{9,11},{10,12},{11,13},... | collective-permute-start | bytes 1572872 | tf_op jit(solution)/shard_map/ppermute | solution.py:34
  905.2 100.8 %collective-permute-start.25 = (bf16[128,2048]{1,0:T(8,128)(2,1)S(1)}, bf16[128,2048]{1,0:T(8,128)(2,1)}, u32[]{:S(2)}, u32[]{:S(2)}) collective-permute-start(bf16[128,2048]{1,0:T(8,128)(2,1)S(1)} %slice.521), channel_id=1, source_target_pairs={{0,3},{1,4},{2,5},{3,6},{4,7},{8,11},{9,12},{10,13},{11,14},{12,15... | collective-permute-start | bytes 1572872 | tf_op jit(solution)/shard_map/ppermute | solution.py:34
  908.1 70.2 %collective-permute-start.23 = (bf16[128,2048]{1,0:T(8,128)(2,1)S(1)}, bf16[128,2048]{1,0:T(8,128)(2,1)S(1)}, u32[]{:S(2)}, u32[]{:S(2)}) collective-permute-start(bf16[128,2048]{1,0:T(8,128)(2,1)S(1)} %slice.521), channel_id=1, source_target_pairs={{0,5},{1,6},{2,7},{8,13},{9,14},{10,15},{16,21},{17,22},{18,23},{2... | collective-permute-start | bytes 1572872 | tf_op jit(solution)/shard_map/ppermute | solution.py:34
  910.2 65.1 %collective-permute-start.22 = (bf16[128,2048]{1,0:T(8,128)(2,1)S(1)}, bf16[128,2048]{1,0:T(8,128)(2,1)S(1)}, u32[]{:S(2)}, u32[]{:S(2)}) collective-permute-start(bf16[128,2048]{1,0:T(8,128)(2,1)S(1)} %slice.521), channel_id=1, source_target_pairs={{0,6},{1,7},{8,14},{9,15},{16,22},{17,23},{24,30},{25,31}} | collective-permute-start | bytes 1572872 | tf_op jit(solution)/shard_map/ppermute | solution.py:34
  912.4 60.8 %collective-permute-start.21 = (bf16[128,2048]{1,0:T(8,128)(2,1)S(1)}, bf16[128,2048]{1,0:T(8,128)(2,1)S(1)}, u32[]{:S(2)}, u32[]{:S(2)}) collective-permute-start(bf16[128,2048]{1,0:T(8,128)(2,1)S(1)} %slice.521), channel_id=1, source_target_pairs={{0,7},{8,15},{16,23},{24,31}} | collective-permute-start | bytes 1572872 | tf_op jit(solution)/shard_map/ppermute | solution.py:34
  975.3 37.9 %collective-permute-start.27 = (bf16[128,2048]{1,0:T(8,128)(2,1)S(1)}, bf16[128,2048]{1,0:T(8,128)(2,1)}, u32[]{:S(2)}, u32[]{:S(2)}) collective-permute-start(bf16[128,2048]{1,0:T(8,128)(2,1)S(1)} %slice.521), channel_id=1, source_target_pairs={{0,1},{1,2},{2,3},{3,4},{4,5},{5,6},{6,7},{8,9},{9,10},{10,11},{11... | collective-permute-start | bytes 1572872 | tf_op jit(solution)/shard_map/ppermute | solution.py:34
  978.3 112.2 %collective-permute-start.32 = (bf16[128,2048]{0,1:T(8,128)(2,1)}, bf16[128,2048]{0,1:T(8,128)(2,1)S(1)}, u32[]{:S(2)}, u32[]{:S(2)}) collective-permute-start(bf16[128,2048]{0,1:T(8,128)(2,1)} %bitcast.37), channel_id=1, source_target_pairs={{0,3},{1,4},{2,5},{3,6},{4,7},{8,11},{9,12},{10,13},{11,14},{12,15... | collective-permute-start | bytes 1572872 | tf_op jit(solution)/shard_map/ppermute | solution.py:34
  993.4 94.9 %collective-permute-start.31 = (bf16[128,2048]{0,1:T(8,128)(2,1)}, bf16[128,2048]{0,1:T(8,128)(2,1)S(1)}, u32[]{:S(2)}, u32[]{:S(2)}) collective-permute-start(bf16[128,2048]{0,1:T(8,128)(2,1)} %bitcast.37), channel_id=1, source_target_pairs={{0,4},{1,5},{2,6},{3,7},{8,12},{9,13},{10,14},{11,15},{16,20},{17,... | collective-permute-start | bytes 1572872 | tf_op jit(solution)/shard_map/ppermute | solution.py:34
  1006.0 79.2 %collective-permute-start.30 = (bf16[128,2048]{0,1:T(8,128)(2,1)}, bf16[128,2048]{0,1:T(8,128)(2,1)}, u32[]{:S(2)}, u32[]{:S(2)}) collective-permute-start(bf16[128,2048]{0,1:T(8,128)(2,1)} %bitcast.37), channel_id=1, source_target_pairs={{0,5},{1,6},{2,7},{8,13},{9,14},{10,15},{16,21},{17,22},{18,23},{2... | collective-permute-start | bytes 1572872 | tf_op jit(solution)/shard_map/ppermute | solution.py:34
  1010.0 61.9 %collective-permute-start.29 = (bf16[128,2048]{0,1:T(8,128)(2,1)}, bf16[128,2048]{0,1:T(8,128)(2,1)S(1)}, u32[]{:S(2)}, u32[]{:S(2)}) collective-permute-start(bf16[128,2048]{0,1:T(8,128)(2,1)} %bitcast.37), channel_id=1, source_target_pairs={{0,6},{1,7},{8,14},{9,15},{16,22},{17,23},{24,30},{25,31}} | collective-permute-start | bytes 1572872 | tf_op jit(solution)/shard_map/ppermute | solution.py:34
  1013.2 55.1 %collective-permute-start.28 = (bf16[128,2048]{0,1:T(8,128)(2,1)}, bf16[128,2048]{0,1:T(8,128)(2,1)S(1)}, u32[]{:S(2)}, u32[]{:S(2)}) collective-permute-start(bf16[128,2048]{0,1:T(8,128)(2,1)} %bitcast.37), channel_id=1, source_target_pairs={{0,7},{8,15},{16,23},{24,31}} | collective-permute-start | bytes 1572872 | tf_op jit(solution)/shard_map/ppermute | solution.py:34
  1068.3 24.2 collective-permute-start.33
  1071.9 23.9 collective-permute-start.34
  1085.2 108.2 %collective-permute-start.41 = (bf16[128,2048]{0,1:T(8,128)(2,1)}, bf16[128,2048]{0,1:T(8,128)(2,1)}, u32[]{:S(2)}, u32[]{:S(2)}) collective-permute-start(bf16[128,2048]{0,1:T(8,128)(2,1)} %bitcast.71), channel_id=1, source_target_pairs={{7,0},{15,8},{23,16},{31,24}} | collective-permute-start | bytes 1572872 | tf_op jit(solution)/shard_map/ppermute | solution.py:34
  1088.3 106.5 %collective-permute-start.35 = (bf16[128,2048]{0,1:T(8,128)(2,1)}, bf16[128,2048]{0,1:T(8,128)(2,1)}, u32[]{:S(2)}, u32[]{:S(2)}) collective-permute-start(bf16[128,2048]{0,1:T(8,128)(2,1)} %bitcast.65), channel_id=1, source_target_pairs={{1,0},{2,1},{3,2},{4,3},{5,4},{6,5},{7,6},{9,8},{10,9},{11,10},{12... | collective-permute-start | bytes 1572872 | tf_op jit(solution)/shard_map/ppermute | solution.py:34
  1090.4 106.7 %collective-permute-start.40 = (bf16[128,2048]{0,1:T(8,128)(2,1)}, bf16[128,2048]{0,1:T(8,128)(2,1)}, u32[]{:S(2)}, u32[]{:S(2)}) collective-permute-start(bf16[128,2048]{0,1:T(8,128)(2,1)} %bitcast.70), channel_id=1, source_target_pairs={{6,0},{7,1},{14,8},{15,9},{22,16},{23,17},{30,24},{31,25}} | collective-permute-start | bytes 1572872 | tf_op jit(solution)/shard_map/ppermute | solution.py:34
  1092.6 105.9 %collective-permute-start.39 = (bf16[128,2048]{0,1:T(8,128)(2,1)}, bf16[128,2048]{0,1:T(8,128)(2,1)}, u32[]{:S(2)}, u32[]{:S(2)}) collective-permute-start(bf16[128,2048]{0,1:T(8,128)(2,1)} %bitcast.69), channel_id=1, source_target_pairs={{5,0},{6,1},{7,2},{13,8},{14,9},{15,10},{21,16},{22,17},{23,18},{2... | collective-permute-start | bytes 1572872 | tf_op jit(solution)/shard_map/ppermute | solution.py:34
  1095.7 104.0 %collective-permute-start.38 = (bf16[128,2048]{0,1:T(8,128)(2,1)}, bf16[128,2048]{0,1:T(8,128)(2,1)}, u32[]{:S(2)}, u32[]{:S(2)}) collective-permute-start(bf16[128,2048]{0,1:T(8,128)(2,1)} %bitcast.68), channel_id=1, source_target_pairs={{4,0},{5,1},{6,2},{7,3},{12,8},{13,9},{14,10},{15,11},{20,16},{21,... | collective-permute-start | bytes 1572872 | tf_op jit(solution)/shard_map/ppermute | solution.py:34
  1197.1 39.5 %collective-permute-start.55 = (bf16[128,2048]{0,1:T(8,128)(2,1)S(1)}, bf16[128,2048]{0,1:T(8,128)(2,1)S(1)}, u32[]{:S(2)}, u32[]{:S(2)}) collective-permute-start(bf16[128,2048]{0,1:T(8,128)(2,1)S(1)} %bitcast.361), channel_id=1, source_target_pairs={{7,0},{15,8},{23,16},{31,24}} | collective-permute-start | bytes 1572872 | tf_op jit(solution)/shard_map/ppermute | solution.py:34
  1198.5 39.5 %collective-permute-start.49 = (bf16[128,2048]{0,1:T(8,128)(2,1)S(1)}, bf16[128,2048]{0,1:T(8,128)(2,1)S(1)}, u32[]{:S(2)}, u32[]{:S(2)}) collective-permute-start(bf16[128,2048]{0,1:T(8,128)(2,1)S(1)} %bitcast.360), channel_id=1, source_target_pairs={{1,0},{2,1},{3,2},{4,3},{5,4},{6,5},{7,6},{9,8},{10,9},{11,10},{12... | collective-permute-start | bytes 1572872 | tf_op jit(solution)/shard_map/ppermute | solution.py:34
  1199.8 39.9 %collective-permute-start.54 = (bf16[128,2048]{0,1:T(8,128)(2,1)S(1)}, bf16[128,2048]{0,1:T(8,128)(2,1)S(1)}, u32[]{:S(2)}, u32[]{:S(2)}) collective-permute-start(bf16[128,2048]{0,1:T(8,128)(2,1)S(1)} %bitcast.359), channel_id=1, source_target_pairs={{6,0},{7,1},{14,8},{15,9},{22,16},{23,17},{30,24},{31,25}} | collective-permute-start | bytes 1572872 | tf_op jit(solution)/shard_map/ppermute | solution.py:34
  1207.2 33.7 %collective-permute-start.53 = (bf16[128,2048]{0,1:T(8,128)(2,1)S(1)}, bf16[128,2048]{0,1:T(8,128)(2,1)S(1)}, u32[]{:S(2)}, u32[]{:S(2)}) collective-permute-start(bf16[128,2048]{0,1:T(8,128)(2,1)S(1)} %bitcast.358), channel_id=1, source_target_pairs={{5,0},{6,1},{7,2},{13,8},{14,9},{15,10},{21,16},{22,17},{23,18},{2... | collective-permute-start | bytes 1572872 | tf_op jit(solution)/shard_map/ppermute | solution.py:34
  1212.1 30.1 %collective-permute-start.52 = (bf16[128,2048]{0,1:T(8,128)(2,1)S(1)}, bf16[128,2048]{0,1:T(8,128)(2,1)S(1)}, u32[]{:S(2)}, u32[]{:S(2)}) collective-permute-start(bf16[128,2048]{0,1:T(8,128)(2,1)S(1)} %bitcast.357), channel_id=1, source_target_pairs={{4,0},{5,1},{6,2},{7,3},{12,8},{13,9},{14,10},{15,11},{20,16},{21,... | collective-permute-start | bytes 1572872 | tf_op jit(solution)/shard_map/ppermute | solution.py:34
  1236.6 23.5 collective-permute-start.51
  1237.9 23.5 collective-permute-start.50
  1239.6 47.4 %collective-permute-start.48 = (bf16[128,2048]{0,1:T(8,128)(2,1)S(1)}, bf16[128,2048]{0,1:T(8,128)(2,1)S(1)}, u32[]{:S(2)}, u32[]{:S(2)}) collective-permute-start(bf16[128,2048]{0,1:T(8,128)(2,1)S(1)} %bitcast.354), channel_id=1, source_target_pairs={{7,0},{15,8},{23,16},{31,24}} | collective-permute-start | bytes 1572872 | tf_op jit(solution)/shard_map/ppermute | solution.py:34
  1240.9 47.4 %collective-permute-start.42 = (bf16[128,2048]{0,1:T(8,128)(2,1)S(1)}, bf16[128,2048]{0,1:T(8,128)(2,1)S(1)}, u32[]{:S(2)}, u32[]{:S(2)}) collective-permute-start(bf16[128,2048]{0,1:T(8,128)(2,1)S(1)} %bitcast.353), channel_id=1, source_target_pairs={{1,0},{2,1},{3,2},{4,3},{5,4},{6,5},{7,6},{9,8},{10,9},{11,10},{12... | collective-permute-start | bytes 1572872 | tf_op jit(solution)/shard_map/ppermute | solution.py:34
  1242.2 48.7 %collective-permute-start.47 = (bf16[128,2048]{0,1:T(8,128)(2,1)S(1)}, bf16[128,2048]{0,1:T(8,128)(2,1)S(1)}, u32[]{:S(2)}, u32[]{:S(2)}) collective-permute-start(bf16[128,2048]{0,1:T(8,128)(2,1)S(1)} %bitcast.351), channel_id=1, source_target_pairs={{6,0},{7,1},{14,8},{15,9},{22,16},{23,17},{30,24},{31,25}} | collective-permute-start | bytes 1572872 | tf_op jit(solution)/shard_map/ppermute | solution.py:34
  1260.1 32.1 %collective-permute-start.46 = (bf16[128,2048]{0,1:T(8,128)(2,1)S(1)}, bf16[128,2048]{0,1:T(8,128)(2,1)S(1)}, u32[]{:S(2)}, u32[]{:S(2)}) collective-permute-start(bf16[128,2048]{0,1:T(8,128)(2,1)S(1)} %bitcast.349), channel_id=1, source_target_pairs={{5,0},{6,1},{7,2},{13,8},{14,9},{15,10},{21,16},{22,17},{23,18},{2... | collective-permute-start | bytes 1572872 | tf_op jit(solution)/shard_map/ppermute | solution.py:34
  1261.4 37.2 %collective-permute-start.45 = (bf16[128,2048]{0,1:T(8,128)(2,1)S(1)}, bf16[128,2048]{0,1:T(8,128)(2,1)S(1)}, u32[]{:S(2)}, u32[]{:S(2)}) collective-permute-start(bf16[128,2048]{0,1:T(8,128)(2,1)S(1)} %bitcast.348), channel_id=1, source_target_pairs={{4,0},{5,1},{6,2},{7,3},{12,8},{13,9},{14,10},{15,11},{20,16},{21,... | collective-permute-start | bytes 1572872 | tf_op jit(solution)/shard_map/ppermute | solution.py:34
  1290.9 41.1 %collective-permute-start.62 = (bf16[128,2048]{0,1:T(8,128)(2,1)S(1)}, bf16[128,2048]{0,1:T(8,128)(2,1)S(1)}, u32[]{:S(2)}, u32[]{:S(2)}) collective-permute-start(bf16[128,2048]{0,1:T(8,128)(2,1)S(1)} %bitcast.345), channel_id=1, source_target_pairs={{7,0},{15,8},{23,16},{31,24}} | collective-permute-start | bytes 1572872 | tf_op jit(solution)/shard_map/ppermute | solution.py:34
  1292.2 41.1 %collective-permute-start.56 = (bf16[128,2048]{0,1:T(8,128)(2,1)S(1)}, bf16[128,2048]{0,1:T(8,128)(2,1)S(1)}, u32[]{:S(2)}, u32[]{:S(2)}) collective-permute-start(bf16[128,2048]{0,1:T(8,128)(2,1)S(1)} %bitcast.344), channel_id=1, source_target_pairs={{1,0},{2,1},{3,2},{4,3},{5,4},{6,5},{7,6},{9,8},{10,9},{11,10},{12... | collective-permute-start | bytes 1572872 | tf_op jit(solution)/shard_map/ppermute | solution.py:34
  1298.6 37.3 %collective-permute-start.61 = (bf16[128,2048]{0,1:T(8,128)(2,1)S(1)}, bf16[128,2048]{0,1:T(8,128)(2,1)S(1)}, u32[]{:S(2)}, u32[]{:S(2)}) collective-permute-start(bf16[128,2048]{0,1:T(8,128)(2,1)S(1)} %bitcast.343), channel_id=1, source_target_pairs={{6,0},{7,1},{14,8},{15,9},{22,16},{23,17},{30,24},{31,25}} | collective-permute-start | bytes 1572872 | tf_op jit(solution)/shard_map/ppermute | solution.py:34
  1301.2 34.7 %collective-permute-start.60 = (bf16[128,2048]{0,1:T(8,128)(2,1)S(1)}, bf16[128,2048]{0,1:T(8,128)(2,1)S(1)}, u32[]{:S(2)}, u32[]{:S(2)}) collective-permute-start(bf16[128,2048]{0,1:T(8,128)(2,1)S(1)} %bitcast.342), channel_id=1, source_target_pairs={{5,0},{6,1},{7,2},{13,8},{14,9},{15,10},{21,16},{22,17},{23,18},{2... | collective-permute-start | bytes 1572872 | tf_op jit(solution)/shard_map/ppermute | solution.py:34
  1305.1 44.4 %collective-permute-start.59 = (bf16[128,2048]{0,1:T(8,128)(2,1)S(1)}, bf16[128,2048]{0,1:T(8,128)(2,1)S(1)}, u32[]{:S(2)}, u32[]{:S(2)}) collective-permute-start(bf16[128,2048]{0,1:T(8,128)(2,1)S(1)} %bitcast.341), channel_id=1, source_target_pairs={{4,0},{5,1},{6,2},{7,3},{12,8},{13,9},{14,10},{15,11},{20,16},{21,... | collective-permute-start | bytes 1572872 | tf_op jit(solution)/shard_map/ppermute | solution.py:34
  1558.8 33.9 %all-to-all-start.3 = ((bf16[2,8,16,2048]{3,2,0,1:T(8,128)(2,1)}), bf16[2,8,16,2048]{3,2,0,1:T(8,128)(2,1)}, u32[]{:S(2)}, u32[]{:S(2)}) async-start(bf16[2,8,16,2048]{3,2,0,1:T(8,128)(2,1)} %pad_maximum_fusion.4), calls=%async_computation.3 | async-start | bytes 2097152 | tf_op jit(solution)/shard_map/all_to_all | solution.py:355
  1592.7 55.3 %all-to-all-start.1 = ((bf16[2,8,16,2048]{3,2,0,1:T(8,128)(2,1)}), bf16[2,8,16,2048]{3,2,0,1:T(8,128)(2,1)S(1)}, u32[]{:S(2)}, u32[]{:S(2)}) async-start(bf16[2,8,16,2048]{3,2,0,1:T(8,128)(2,1)} %pad_maximum_fusion.3), calls=%async_computation.1 | async-start | bytes 2097152 | tf_op jit(solution)/shard_map/all_to_all | solution.py:354
  (139 other events, 6678.3 us)
Sparse Core Ops, SparseCore 0:
  9.9 90.1 all-gather.10
  102.0 225.1 all-gather.8
  329.1 248.0 all-gather.12
  737.8 314.1 reduce-scatter.4
  1426.6 419.2 reduce-scatter.2
